TPU v7x, 32 devices: a whole 2x2x4 slice. The times are simulated.
32 devices in a mesh: ens: 2 (over x), gx: 16 (over z, y, core).
Axes of the slice: x: 2, y: 2, z: 4, core: 2. Of those that a mesh axis runs over, the one named last changes fastest.
Arguments:
- vectors: float32 [64, 64, 96, 128], P(None, ('ens', 'gx')), parts along dimension 1, may hold values from -45 to 45
- stream_speed: float32 [64, 96, 128], P(('ens', 'gx')), parts along dimension 0, may hold values from 0.5 to 1.5
- span_speed: float32 [64, 96, 128], P(('ens', 'gx')), parts along dimension 0, may hold values from -0.5 to 0.5
- damping: float32 [64, 96, 128], P(('ens', 'gx')), parts along dimension 0, may hold values from -0.5 to 0.5
Outputs:
- basis: float32 [64, 64, 96, 128], P(None, ('ens', 'gx')), parts along dimension 1
- growth: float32 [128], P('ens'), parts along dimension 0
There are 2 independent parts, one for each index of `ens`. A program takes and returns all parts, laid end to end along the dimension named above; each array names one. Nothing has to cross between parts.
All inputs are finite; a program needn't handle non-finite values.
Results may differ from a plain program's by a relative error of at most 0.00055.
Values sent between devices are 32-bit elements; how exact they have to be, the bound alone decides.
No kernel may reach another device: no remote copies, remote signals or barrier semaphores. Data moves between devices by JAX's collectives and lax.ppermute only.
A program may use at most 256 MiB of HBM per device.

v0:
```python
import functools
import math

import jax
import jax.numpy as jnp
from jax import lax
from jax.experimental import pallas as pl
from jax.experimental.pallas import tpu as pltpu
from jax.sharding import PartitionSpec as P

HIGH = lax.Precision.HIGHEST
F32 = jnp.float32
BF16 = jnp.bfloat16
ROWS = 8
UNROLL = 8
FUSED = 5
HOP_EVERY = 1
STEP = 0.3
MIX = 0.05
VMEM_LIMIT = 24 * 1024 * 1024


def shift(block, axis, step):
    count = lax.axis_size(axis)
    return lax.ppermute(block, axis, [(i, (i + step) % count) for i in range(count)])


def exchange(value, axis, hop):
    return lax.ppermute(value, axis, [(i, i ^ hop) for i in range(lax.axis_size(axis))])


def group_sum(value, axis):
    hop = 1
    while hop < lax.axis_size(axis):
        value = value + exchange(value, axis, hop)
        hop *= 2
    return value


def spectral_tables(points):
    indices = jnp.arange(points, dtype=jnp.int32)
    offset = indices[:, None] - indices[None, :]
    parity = (1 - 2 * ((offset + points) % 2)).astype(F32)
    spacing = 2.0 * math.pi / points
    diagonal_mask = offset == 0
    angles = jnp.where(diagonal_mask, 1, offset).astype(F32) * (spacing / 2.0)
    derivative = (
        jnp.where(diagonal_mask, 0.0, 0.5 * parity * jnp.cos(angles) / jnp.sin(angles)) * spacing
    )
    curvature = jnp.where(
        diagonal_mask,
        -math.pi**2 / 3.0 - spacing * spacing / 6.0,
        -parity / (2.0 * jnp.sin(angles) ** 2) * spacing * spacing,
    )
    return jnp.concatenate([derivative.T, curvature.T], axis=1)


def pieces(value):
    high = value.astype(BF16)
    rest = value - high.astype(F32)
    middle = rest.astype(BF16)
    low = (rest - middle.astype(F32)).astype(BF16)
    return high, middle, low


def host_pieces(value):
    high = lax.reduce_precision(value, 8, 7)
    middle = lax.reduce_precision(value - high, 8, 7)
    low = (value - high) - middle
    return high.astype(BF16), middle.astype(BF16), low.astype(BF16)


def dot_nt(left, right, precision=None):
    return lax.dot_general(
        left, right, (((1,), (1,)), ((), ())), precision=precision, preferred_element_type=F32
    )


def repeat(start, stop, body):
    groups = (stop - start) // UNROLL
    if groups > 1:

        def several(group, carry):
            for inner in range(UNROLL):
                body(start + group * UNROLL + inner)
            return carry

        lax.fori_loop(0, groups, several, 0)
        start += groups * UNROLL
    for row in range(start, stop):
        body(row)


def turn_kernel(start, vectors_ref, turned_ref, block_ref, sem):
    count, planes, rows, points = block_ref.shape
    copy = pltpu.make_async_copy(vectors_ref.at[:, :, pl.ds(start, rows), :], block_ref, sem)
    copy.start()
    copy.wait()
    flat = block_ref.reshape(count * planes * rows, points)
    for row in range(rows):
        for plane in range(planes):
            turned_ref[plane, row] = flat[
                pl.ds(plane * rows + row, count, stride=planes * rows), :
            ]


def turn(vectors, start, rows):
    count, planes, height, points = vectors.shape
    return pl.pallas_call(
        functools.partial(turn_kernel, start),
        in_specs=[pl.BlockSpec(memory_space=pltpu.HBM)],
        out_specs=pl.BlockSpec(memory_space=pltpu.VMEM),
        scratch_shapes=[
            pltpu.VMEM((count, planes, rows, points), F32),
            pltpu.SemaphoreType.DMA,
        ],
        out_shape=jax.ShapeDtypeStruct((planes, rows, count, points), F32),
        compiler_params=pltpu.CompilerParams(vmem_limit_bytes=8 * 1024 * 1024),
        cost_estimate=pl.CostEstimate(
            flops=0, bytes_accessed=8 * count * planes * rows * points, transcendentals=0
        ),
        name="turn",
    )(vectors)


def gram_kernel(vectors_ref, gram_ref, slots, sems):
    count, planes, height, points = vectors_ref.shape
    steps = height // ROWS

    def fetch(step):
        return pltpu.make_async_copy(
            vectors_ref.at[:, :, pl.ds(pl.multiple_of(step * ROWS, ROWS), ROWS), :],
            slots.at[step % 2],
            sems.at[step % 2],
        )

    gram_ref[...] = jnp.zeros_like(gram_ref)
    fetch(0).start()

    def body(step, carry):
        @pl.when(step + 1 < steps)
        def _():
            fetch(step + 1).start()

        fetch(step).wait()
        flat = slots.at[step % 2].reshape(count * planes * ROWS, points)
        total = jnp.zeros((count, count), F32)
        for row in range(ROWS):
            both = jnp.concatenate(
                [
                    flat[pl.ds(plane * ROWS + row, count, stride=planes * ROWS), :]
                    for plane in range(planes)
                ],
                axis=1,
            )
            total += dot_nt(both, both, HIGH)
        gram_ref[...] += total
        return carry

    lax.fori_loop(0, steps, body, 0)


def gram_of(vectors):
    count, planes, height, points = vectors.shape
    return pl.pallas_call(
        gram_kernel,
        in_specs=[pl.BlockSpec(memory_space=pltpu.HBM)],
        out_specs=pl.BlockSpec(memory_space=pltpu.VMEM),
        out_shape=jax.ShapeDtypeStruct((count, count), F32),
        scratch_shapes=[
            pltpu.VMEM((2, count, planes, ROWS, points), F32),
            pltpu.SemaphoreType.DMA((2,)),
        ],
        compiler_params=pltpu.CompilerParams(vmem_limit_bytes=16 * 1024 * 1024),
        cost_estimate=pl.CostEstimate(
            flops=12 * vectors.size * count, bytes_accessed=4 * vectors.size, transcendentals=0
        ),
        name="gram",
    )(vectors)


def factor_kernel(scale, *refs):
    gram_ref, before_ref = refs[0], refs[1] if len(refs) > 4 else None
    left_ref, logs_ref, upper_ref = refs[-3:]
    count = gram_ref.shape[1]
    rows = lax.broadcasted_iota(jnp.int32, (count, count), 0)
    lanes = lax.broadcasted_iota(jnp.int32, (count, count), 1)
    tile = 8
    gram = gram_ref[...] * scale
    work = jnp.concatenate([gram, jnp.where(rows == lanes, 1.0, 0.0).astype(F32)], axis=1)
    blocks = [work[i : i + tile] for i in range(0, count, tile)]
    for j in range(count):
        here, inner = divmod(j, tile)
        row = blocks[here][inner : inner + 1]
        root = lax.rsqrt(row[:, j : j + 1])
        scaled = row * root
        upper_ref[j : j + 1, :] = scaled
        row_all = jnp.broadcast_to(scaled, (tile, 2 * count))
        for b in range(here, len(blocks)):
            blocks[b] = blocks[b] - (blocks[b][:, j : j + 1] * root) * row_all
    upper = upper_ref[...]
    left_ref[...] = split_six_left(upper[:, count:])
    diagonal = jnp.where(rows == lanes, upper[:, :count], 0.0)
    logs = jnp.log(jnp.sum(diagonal, axis=0, keepdims=True))
    logs_ref[...] = logs if before_ref is None else logs + before_ref[...]


def factor(gram, total, before=None):
    count = gram.shape[0]
    operands = [gram] + ([] if before is None else [before])
    return pl.pallas_call(
        functools.partial(factor_kernel, 1.0 / total),
        out_shape=[
            jax.ShapeDtypeStruct((count, 6 * count), BF16),
            jax.ShapeDtypeStruct((1, count), F32),
        ],
        scratch_shapes=[pltpu.VMEM((count, 2 * count), F32)],
        compiler_params=pltpu.CompilerParams(vmem_limit_bytes=4 * 1024 * 1024),
        name="factor",
    )(*operands)


def split_six_right(value):
    high, middle, low = pieces(value)
    return jnp.concatenate([high, middle, high, middle, low, high], axis=0)


def split_six_left(value):
    high, middle, low = pieces(value)
    return jnp.concatenate([high, high, middle, middle, high, low], axis=1)


def mix_kernel(start, stop, mixer_ref, _, *refs):
    basis_ref, gram_ref = refs[-2:]
    gram_ref[...] = refs[0][...] if len(refs) > 2 else jnp.zeros_like(gram_ref)
    points = basis_ref.shape[3]

    def group(first, rows):
        sides = []
        for row in range(rows):
            advanced = jnp.concatenate(
                [basis_ref[first + row, 0], basis_ref[first + row, 1]], axis=1
            )
            mixed = jnp.dot(
                mixer_ref[...], split_six_right(advanced), preferred_element_type=F32
            )
            for plane in range(2):
                basis_ref[first + row, plane] = mixed[:, plane * points : (plane + 1) * points]
            high = mixed.astype(BF16)
            rest = (mixed - high.astype(F32)).astype(BF16)
            sides.append(jnp.concatenate([high, rest], axis=0))
        sides = jnp.concatenate(sides, axis=1)
        gram_ref[...] += dot_nt(sides, sides)

    groups = (stop - start) // UNROLL
    if groups > 1:

        def several(index, carry):
            group(start + index * UNROLL, UNROLL)
            return carry

        lax.fori_loop(0, groups, several, 0)
        start += groups * UNROLL
    if stop > start:
        group(start, stop - start)


def mix(start, stop, mixer, basis, gram):
    height, planes, count, points = basis.shape
    memory = pl.BlockSpec(memory_space=pltpu.VMEM)
    operands = [mixer, basis] + ([] if gram is None else [gram])
    return pl.pallas_call(
        functools.partial(mix_kernel, start, stop),
        in_specs=[memory] * len(operands),
        out_specs=[memory, memory],
        out_shape=[
            jax.ShapeDtypeStruct(basis.shape, F32),
            jax.ShapeDtypeStruct((2 * count, 2 * count), F32),
        ],
        input_output_aliases={1: 0},
        compiler_params=pltpu.CompilerParams(vmem_limit_bytes=8 * 1024 * 1024),
        cost_estimate=pl.CostEstimate(
            flops=(stop - start) * count * planes * points * count * 20,
            bytes_accessed=8 * (stop - start) * count * planes * points,
            transcendentals=0,
        ),
        name="mix",
    )(*operands)


def advance_kernel(first, last, base, *refs):
    refs = list(refs)
    tables_ref, coefs_ref, own_ref, low_ref, high_ref = refs[:5]
    refs = refs[5:]
    if not first:
        own_old_ref, low_old_ref, high_old_ref, state_in_ref, _ = refs[:5]
        refs = refs[5:]
    basis_ref = refs.pop(0)
    if not last:
        state_ref = refs.pop(0)
    field, stage, coef = refs
    rows, count, points = own_ref.shape[1:]
    start = 2 if first else 0
    stop = rows + 2 if last else rows
    zeros = jnp.zeros((count, points), F32)

    for plane in range(2):
        if first:
            for j in range(2):
                field[j, plane] = zeros
                field[j, 2 + plane] = zeros
                field[j, 4 + plane] = zeros
        else:
            field[0:2, plane] = low_old_ref[plane]
            field[0:2, 2 + plane] = own_old_ref[plane]
            field[0:2, 4 + plane] = high_old_ref[plane]
        field[2 : 2 + rows, plane] = low_ref[plane]
        field[2 : 2 + rows, 2 + plane] = own_ref[plane]
        field[2 : 2 + rows, 4 + plane] = high_ref[plane]
        if last:
            for q in range(3):
                field[2 + rows, 2 * q + plane] = zeros
    if first:
        for q in range(4):
            stage[2, q] = zeros
    else:
        stage[0:2] = state_in_ref[...]
        coef[0:2] = coefs_ref[base : base + 2]
    coef[2 : 2 + rows] = coefs_ref[base + 2 : base + 2 + rows]
    if last:
        for q in range(4):
            stage[rows + 3, q] = zeros
    tables = tables_ref[...]

    def spanwise(values):
        high, middle, low = pieces(values)
        left = jnp.concatenate([high, middle, high, middle, low, high], axis=1)
        return jnp.dot(left, tables, preferred_element_type=F32)

    def slope(center, ahead, behind, above, below, product, row, q):
        c = coef[row, pl.ds(q * 4, 4), :]
        return (
            c[0:1] * ahead
            + c[1:2] * behind
            + c[2:3] * product[:, :points]
            + product[:, points:]
            + (STEP * MIX) * (above + below)
            + c[3:4] * center
        )

    def first_stage(i):
        middle_row = i - 1
        center = field[middle_row, 1:5].reshape(4 * count, points)
        product = spanwise(center)
        for q in range(4):
            mine = field[middle_row, 1 + q]
            stage[i, q] = mine + slope(
                mine,
                field[middle_row, 2 + q],
                field[middle_row, q],
                field[i, 1 + q],
                field[i - 2, 1 + q],
                product[q * count : (q + 1) * count],
                middle_row,
                q,
            )

    def second_stage(m):
        center = stage[m + 1, 1:3].reshape(2 * count, points)
        product = spanwise(center)
        results = []
        for q in range(1, 3):
            mine = stage[m + 1, q]
            value = mine + slope(
                mine,
                stage[m + 1, q + 1],
                stage[m + 1, q - 1],
                stage[m + 2, q],
                stage[m, q],
                product[(q - 1) * count : q * count],
                m,
                q,
            )
            results.append(0.75 * field[m, 1 + q] + 0.25 * value)
        for plane in range(2):
            basis_ref[base + m, plane] = results[plane]

    repeat(3 if first else 2, rows + 3 if last else rows + 2, first_stage)
    repeat(start, stop, second_stage)
    if not last:
        state_ref[...] = stage[rows : rows + 2]


def advance(index, base, height, tables, coefs, own, low, high, state, basis):
    planes, rows, count, points = own[index].shape
    first, last = index == 0, base + rows == height
    memory = pl.BlockSpec(memory_space=pltpu.VMEM)

    def whole(shape):
        return pl.BlockSpec(shape, lambda i: (0,) * len(shape))

    block = whole((planes, rows, count, points))
    before = 0 if first else own[index - 1].shape[1]
    tail = pl.BlockSpec((planes, 2, count, points), lambda i: (0, before // 2 - 1, 0, 0))
    operands = [tables, coefs, own[index], low[index], high[index]]
    specs = [memory, memory, block, block, block]
    aliases = {}
    if not first:
        operands += [own[index - 1], low[index - 1], high[index - 1], state, basis]
        specs += [tail, tail, tail, whole((2, 4, count, points)), memory]
        aliases = {len(operands) - 1: 0}
    out_specs = [memory]
    out_shape = [jax.ShapeDtypeStruct((height, planes, count, points), F32)]
    if not last:
        out_specs.append(whole((2, 4, count, points)))
        out_shape.append(jax.ShapeDtypeStruct((2, 4, count, points), F32))
    results = pl.pallas_call(
        functools.partial(advance_kernel, first, last, base - 2),
        grid=(1,),
        in_specs=specs,
        out_specs=out_specs,
        out_shape=out_shape,
        scratch_shapes=[
            pltpu.VMEM((rows + 3, 6, count, points), F32),
            pltpu.VMEM((rows + 4, 4, count, points), F32),
            pltpu.VMEM((rows + 2, 16, points), F32),
        ],
        input_output_aliases=aliases,
        compiler_params=pltpu.CompilerParams(vmem_limit_bytes=VMEM_LIMIT),
        cost_estimate=pl.CostEstimate(
            flops=rows * count * points * 6 * 2 * 1000,
            bytes_accessed=4 * rows * count * points * 8,
            transcendentals=0,
        ),
        name="advance",
    )(*operands)
    return results[0], None if last else results[1]


def finish_kernel(inverse_ref, partial_ref, basis_ref, slots, sems):
    _, planes, count, rows, points = slots.shape
    steps = partial_ref.shape[0] // rows
    left = inverse_ref[:, : 4 * count]

    def copies(step):
        return [
            pltpu.make_async_copy(
                slots.at[step % 2, plane],
                basis_ref.at[:, plane, pl.ds(pl.multiple_of(step * rows, 8), rows), :],
                sems.at[step % 2, plane],
            )
            for plane in range(planes)
        ]

    def body(step, carry):
        @pl.when(step >= 2)
        def _():
            for copy in copies(step - 2):
                copy.wait()

        flats = [
            slots.at[step % 2, plane].reshape(count * rows, points) for plane in range(planes)
        ]
        for row in range(rows):
            where = step * rows + row
            both = jnp.concatenate([partial_ref[where, 0], partial_ref[where, 1]], axis=1)
            upper = both.astype(BF16)
            lower = (both - upper.astype(F32)).astype(BF16)
            right = jnp.concatenate([upper, lower, upper, lower], axis=0)
            result = jnp.dot(left, right, preferred_element_type=F32)
            for plane in range(planes):
                flats[plane][pl.ds(row, count, stride=rows), :] = result[
                    :, plane * points : (plane + 1) * points
                ]
        for copy in copies(step):
            copy.start()
        return carry

    lax.fori_loop(0, steps, body, 0)
    for step in range(max(steps - 2, 0), steps):
        for copy in copies(step):
            copy.wait()


def finish(inverse, partial_basis):
    height, planes, count, points = partial_basis.shape
    rows = next(rows for rows in (24, 16, 8) if height % rows == 0)
    memory = pl.BlockSpec(memory_space=pltpu.VMEM)
    return pl.pallas_call(
        finish_kernel,
        in_specs=[memory, memory],
        out_specs=pl.BlockSpec(memory_space=pltpu.HBM),
        out_shape=jax.ShapeDtypeStruct((count, planes, height, points), F32),
        scratch_shapes=[
            pltpu.VMEM((2, planes, count, rows, points), F32),
            pltpu.SemaphoreType.DMA((2, planes)),
        ],
        compiler_params=pltpu.CompilerParams(vmem_limit_bytes=12 * 1024 * 1024),
        name="finish",
    )(inverse, partial_basis)


def chunk_rows(height):
    return [ROWS] * (height // ROWS)


def coefficient_rows(stream_speed, span_speed, damping):
    stacked = jnp.stack([stream_speed, span_speed, damping], axis=1)
    stream, span, damp = (
        lax.squeeze(part, [1])
        for part in jnp.split(
            jnp.concatenate(
                [shift(stacked[-1:], "gx", 1), stacked, shift(stacked[:1], "gx", -1)], axis=0
            ),
            3,
            axis=1,
        )
    )
    kinds = jnp.stack(
        [
            STEP * (MIX - 0.5 * stream),
            STEP * (MIX + 0.5 * stream),
            -STEP * span,
            -STEP * (4.0 * MIX + damp),
        ]
    )
    kinds = jnp.transpose(kinds, (2, 1, 0, 3))
    return kinds.reshape(kinds.shape[0], 16, kinds.shape[3])


def gated(value, gate):
    return lax.optimization_barrier((value, gate))[0]


def per_device(vectors, stream_speed, span_speed, damping):
    count, planes, height, points = vectors.shape
    members = lax.axis_size("gx")
    total = planes * height * points * members
    table = spectral_tables(points) * jnp.where(jnp.arange(2 * points) < points, 1.0, STEP * MIX)
    t_high, t_middle, t_low = host_pieces(table)
    tables = jnp.concatenate([t_high, t_high, t_middle, t_middle, t_high, t_low], axis=0)
    sizes = chunk_rows(height)
    starts = [sum(sizes[:index]) for index in range(len(sizes))]
    own, low, high = [], [], []

    def send(gate=None):
        index = len(own)
        if index == len(sizes):
            return
        turned = turn(vectors, starts[index], sizes[index])
        if gate is not None:
            turned = gated(turned, gate)
        own.append(turned)
        low.append(shift(turned, "gx", 1))
        high.append(shift(turned, "gx", -1))

    coefs = coefficient_rows(stream_speed, span_speed, damping)
    send()
    send()
    gram = gram_of(vectors)
    send(gram)
    hops = [1 << k for k in range((members - 1).bit_length())]
    gram = gram + exchange(gram, "gx", hops.pop(len(hops) > 1))
    coefs = gated(coefs, gram)
    mixed_gram = state = basis = None
    mixed = 0
    for index, start in enumerate(starts):
        if index == FUSED:
            for hop in hops:
                gram = gram + exchange(gram, "gx", hop)
            gram = gated(gram, state)
            mixer, logs = factor(gram, total)
        if 0 < index < FUSED and index % HOP_EVERY == 0:
            state = gated(state, gram)
        basis, state = advance(
            index, start, height, tables, coefs, own, low, high, state, basis
        )
        if index < FUSED and index % HOP_EVERY == 0 and hops:
            gram = gated(gram, state)
            gram = gram + exchange(gram, "gx", hops.pop(0))
        if index >= FUSED:
            ready = height if state is None else start + sizes[index] - 2
            basis, mixed_gram = mix(mixed, ready, mixer, basis, mixed_gram)
            mixed = ready
        if state is not None:
            send(state)
    gram = mixed_gram
    gram = gram[:count, :count] + gram[:count, count:] + gram[count:, :count] + gram[count:, count:]
    inverse, logs = factor(group_sum(gram, "gx"), total, logs)
    basis = finish(inverse, basis)
    growth = logs.reshape(count)
    return (basis, growth)


def solution(mesh):
    placed = (
        P(None, ("ens", "gx"), None, None),
        P(("ens", "gx"), None, None),
        P(("ens", "gx"), None, None),
        P(("ens", "gx"), None, None),
    )
    return jax.shard_map(
        per_device,
        mesh=mesh,
        in_specs=placed,
        out_specs=(P(None, ("ens", "gx"), None, None), P("ens")),
        check_vma=False,
    )
```

profile of v0, /device:TPU:0, one launch (start us, length us, event | category | flops | bytes accessed | tf_op | source)
XLA Modules:
  0.0 179.4 jit_solution(17809250176975751258)
XLA Ops:
  0.6 2.8 %copy-done = f32[64,2,96,128]{3,2,1,0:T(8,128)S(1)} copy-done((f32[64,2,96,128]{3,2,1,0:T(8,128)S(1)}, f32[64,2,96,128]{3,2,1,0:T(8,128)}, u32[]{:S(2)}) %copy-start) | copy-done | bytes 6291480
  3.4 0.2 turn.12.refs_2_.refs_5_
  3.7 0.5 collective-permute-start.3
  4.2 5.1 %collective-permute-start.4 = (f32[2,8,64,128]{3,2,1,0:T(8,128)S(1)}, f32[2,8,64,128]{3,2,1,0:T(8,128)S(1)}, u32[]{:S(2)}, u32[]{:S(2)}) collective-permute-start(f32[2,8,64,128]{3,2,1,0:T(8,128)S(1)} %turn.12.refs_2_.refs_5_), channel_id=1, source_target_pairs={{0,15},{1,0},{2,1},{3,2},{4,3},{5,4},{6,5},{7,6},{8,7},{9,8},{10,9... | collective-permute-start | bytes 1572872 | tf_op jit(solution)/shard_map/ppermute | solution.py:25
  9.4 4.4 %collective-permute-start.2 = (f32[1,3,96,128]{3,2,0,1:T(8,128)S(1)}, f32[1,3,96,128]{3,2,0,1:T(8,128)S(1)}, u32[]{:S(2)}, u32[]{:S(2)}) collective-permute-start(f32[1,3,96,128]{3,2,0,1:T(8,128)S(1)} %get-tuple-element.127), channel_id=1, source_target_pairs={{0,15},{1,0},{2,1},{3,2},{4,3},{5,4},{6,5},{7,6},{8,7},{9,8},{10,9... | collective-permute-start | bytes 442376 | tf_op jit(solution)/shard_map/ppermute | solution.py:25
  13.8 8.1 %gram.1 = f32[64,64]{1,0:T(8,128)S(1)} custom-call(f32[64,2,96,128]{3,2,1,0:T(8,128)S(1)} %copy-done.1), custom_call_target="tpu_custom_call" | custom-call | flops 1207959552 | bytes 6291456 | tf_op jit(solution)/shard_map/gram/pallas_call | solution.py:165
  22.0 0.3 multiply_select_fusion
  22.5 0.2 turn.13.refs_2_.refs_5_
  22.7 0.2 turn.14.refs_2_.refs_5_
  23.0 2.9 %collective-permute-done = f32[64,64]{1,0:T(8,128)S(1)} collective-permute-done((f32[64,64]{1,0:T(8,128)S(1)}, f32[64,64]{1,0:T(8,128)S(1)}, u32[]{:S(2)}, u32[]{:S(2)}) %collective-permute-start) | collective-permute-done | bytes 16416 | tf_op jit(solution)/shard_map/ppermute | solution.py:29
  25.9 4.5 %collective-permute-start.7 = (f32[2,8,64,128]{3,2,1,0:T(8,128)S(1)}, f32[2,8,64,128]{3,2,1,0:T(8,128)S(1)}, u32[]{:S(2)}, u32[]{:S(2)}) collective-permute-start(f32[2,8,64,128]{3,2,1,0:T(8,128)S(1)} %turn.13.refs_2_.refs_5_), channel_id=1, source_target_pairs={{0,15},{1,0},{2,1},{3,2},{4,3},{5,4},{6,5},{7,6},{8,7},{9,8},{10,9... | collective-permute-start | bytes 1572872 | tf_op jit(solution)/shard_map/ppermute | solution.py:25
  30.7 0.5 copy.24
  31.2 0.5 collective-permute-start.9
  31.7 1.3 advance.12
  33.4 0.9 collective-permute-done.5
  34.5 2.8 %collective-permute-done.6.refs_3_.refs_6_ = f32[2,8,64,128]{3,2,1,0:T(8,128)S(1)} collective-permute-done((f32[2,8,64,128]{3,2,1,0:T(8,128)S(1)}, f32[2,8,64,128]{3,2,1,0:T(8,128)S(1)}, u32[]{:S(2)}, u32[]{:S(2)}) %collective-permute-start.6) | collective-permute-done | bytes 524320 | tf_op jit(solution)/shard_map/ppermute | solution.py:25
  37.3 1.5 collective-permute-start.15
  38.9 1.6 advance.13
  40.5 0.2 turn.15.refs_2_.refs_5_
  40.8 8.0 %collective-permute-done.8 = f32[64,64]{1,0:T(8,128)S(1)} collective-permute-done((f32[64,64]{1,0:T(8,128)S(1)}, f32[64,64]{1,0:T(8,128)S(1)}, u32[]{:S(2)}, u32[]{:S(2)}) %collective-permute-start.8) | collective-permute-done | bytes 16416 | tf_op jit(solution)/shard_map/ppermute | solution.py:29
  48.7 7.2 %collective-permute-start.12 = (f32[2,8,64,128]{3,2,1,0:T(8,128)S(1)}, f32[2,8,64,128]{3,2,1,0:T(8,128)S(1)}, u32[]{:S(2)}, u32[]{:S(2)}) collective-permute-start(f32[2,8,64,128]{3,2,1,0:T(8,128)S(1)} %turn.15.refs_2_.refs_5_), channel_id=1, source_target_pairs={{0,1},{1,2},{2,3},{3,4},{4,5},{5,6},{6,7},{7,8},{8,9},{9,10},{10,1... | collective-permute-start | bytes 1572872 | tf_op jit(solution)/shard_map/ppermute | solution.py:25
  56.1 1.6 advance.14
  57.7 1.6 collective-permute-start.11
  59.5 6.3 %collective-permute-done.11 = f32[64,64]{1,0:T(8,128)S(1)} collective-permute-done((f32[64,64]{1,0:T(8,128)S(1)}, f32[64,64]{1,0:T(8,128)S(1)}, u32[]{:S(2)}, u32[]{:S(2)}) %collective-permute-start.11) | collective-permute-done | bytes 16416 | tf_op jit(solution)/shard_map/ppermute | solution.py:29
  65.9 2.2 %collective-permute-start.16 = (f32[2,8,64,128]{3,2,1,0:T(8,128)S(1)}, f32[2,8,64,128]{3,2,1,0:T(8,128)S(1)}, u32[]{:S(2)}, u32[]{:S(2)}) collective-permute-start(f32[2,8,64,128]{3,2,1,0:T(8,128)S(1)} %turn.19.refs_2_.refs_5_), channel_id=1, source_target_pairs={{0,1},{1,2},{2,3},{3,4},{4,5},{5,6},{6,7},{7,8},{8,9},{9,10},{10,1... | collective-permute-start | bytes 1572872 | tf_op jit(solution)/shard_map/ppermute | solution.py:25
  68.1 2.2 %collective-permute-start.17 = (f32[2,8,64,128]{3,2,1,0:T(8,128)S(1)}, f32[2,8,64,128]{3,2,1,0:T(8,128)S(1)}, u32[]{:S(2)}, u32[]{:S(2)}) collective-permute-start(f32[2,8,64,128]{3,2,1,0:T(8,128)S(1)} %turn.19.refs_2_.refs_5_), channel_id=1, source_target_pairs={{0,15},{1,0},{2,1},{3,2},{4,3},{5,4},{6,5},{7,6},{8,7},{9,8},{10,9... | collective-permute-start | bytes 1572872 | tf_op jit(solution)/shard_map/ppermute | solution.py:25
  70.6 1.6 advance.15
  72.2 0.7 collective-permute-start.22
  72.9 3.8 %collective-permute-start.23 = (f32[2,8,64,128]{3,2,1,0:T(8,128)S(1)}, f32[2,8,64,128]{3,2,1,0:T(8,128)S(1)}, u32[]{:S(2)}, u32[]{:S(2)}) collective-permute-start(f32[2,8,64,128]{3,2,1,0:T(8,128)S(1)} %turn.21.refs_2_.refs_5_), channel_id=1, source_target_pairs={{0,15},{1,0},{2,1},{3,2},{4,3},{5,4},{6,5},{7,6},{8,7},{9,8},{10,9... | collective-permute-start | bytes 1572872 | tf_op jit(solution)/shard_map/ppermute | solution.py:25
  76.9 0.2 turn.18.refs_2_.refs_5_
  77.2 0.2 turn.23.refs_2_.refs_5_
  77.5 1.6 advance.16
  79.1 5.4 %factor.2 = (bf16[64,384]{1,0:T(8,128)(2,1)S(1)}, f32[1,64]{1,0:T(1,128)S(1)}) custom-call(f32[64,64]{1,0:T(8,128)S(1)} %add.87.refs_0_), custom_call_target="tpu_custom_call" | custom-call | tf_op jit(solution)/shard_map/factor/pallas_call | solution.py:211
  84.4 7.8 %collective-permute-start.20 = (f32[2,8,64,128]{3,2,1,0:T(8,128)S(1)}, f32[2,8,64,128]{3,2,1,0:T(8,128)S(1)}, u32[]{:S(2)}, u32[]{:S(2)}) collective-permute-start(f32[2,8,64,128]{3,2,1,0:T(8,128)S(1)} %turn.20.refs_2_.refs_5_), channel_id=1, source_target_pairs={{0,1},{1,2},{2,3},{3,4},{4,5},{5,6},{6,7},{7,8},{8,9},{9,10},{10,1... | collective-permute-start | bytes 1572872 | tf_op jit(solution)/shard_map/ppermute | solution.py:25
  92.3 1.6 advance.17
  93.9 4.3 %collective-permute-start.18 = (f32[2,8,64,128]{3,2,1,0:T(8,128)S(1)}, f32[2,8,64,128]{3,2,1,0:T(8,128)S(1)}, u32[]{:S(2)}, u32[]{:S(2)}) collective-permute-start(f32[2,8,64,128]{3,2,1,0:T(8,128)S(1)} %turn.18.refs_2_.refs_5_), channel_id=1, source_target_pairs={{0,1},{1,2},{2,3},{3,4},{4,5},{5,6},{6,7},{7,8},{8,9},{9,10},{10,1... | collective-permute-start | bytes 1572872 | tf_op jit(solution)/shard_map/ppermute | solution.py:25
  98.1 3.6 %mix.7 = (f32[96,2,64,128]{3,2,1,0:T(8,128)S(1)}, f32[128,128]{1,0:T(8,128)S(1)}) custom-call(bf16[64,384]{1,0:T(8,128)(2,1)S(1)} %get-tuple-element.82.mixer_ref, f32[96,2,64,128]{3,2,1,0:T(8,128)S(1)} %get-tuple-element.89._), custom_call_target="tpu_custom_call", output_to_operand_aliasing={{0}: (1, {})} | custom-call | flops 964689920 | bytes 6029312 | tf_op jit(solution)/shard_map/mix/pallas_call | solution.py:272
  101.7 0.3 collective-permute-start.19
  102.0 1.6 advance.18
  103.6 5.8 %collective-permute-start.28 = (f32[2,8,64,128]{3,2,1,0:T(8,128)S(1)}, f32[2,8,64,128]{3,2,1,0:T(8,128)S(1)}, u32[]{:S(2)}, u32[]{:S(2)}) collective-permute-start(f32[2,8,64,128]{3,2,1,0:T(8,128)S(1)} %turn.23.refs_2_.refs_5_), channel_id=1, source_target_pairs={{0,1},{1,2},{2,3},{3,4},{4,5},{5,6},{6,7},{7,8},{8,9},{9,10},{10,1... | collective-permute-start | bytes 1572872 | tf_op jit(solution)/shard_map/ppermute | solution.py:25
  109.6 0.2 turn.17.refs_2_
  110.0 0.6 mix.8
  110.6 1.6 advance.19
  112.2 8.4 %collective-permute-start.26 = (f32[2,8,64,128]{3,2,1,0:T(8,128)S(1)}, f32[2,8,64,128]{3,2,1,0:T(8,128)S(1)}, u32[]{:S(2)}, u32[]{:S(2)}) collective-permute-start(f32[2,8,64,128]{3,2,1,0:T(8,128)S(1)} %turn.22.refs_2_.refs_5_), channel_id=1, source_target_pairs={{0,1},{1,2},{2,3},{3,4},{4,5},{5,6},{6,7},{7,8},{8,9},{9,10},{10,1... | collective-permute-start | bytes 1572872 | tf_op jit(solution)/shard_map/ppermute | solution.py:25
  120.6 0.6 mix.9
  121.2 1.6 advance.20
  122.8 14.6 %collective-permute-start.24 = (f32[2,8,64,128]{3,2,1,0:T(8,128)S(1)}, f32[2,8,64,128]{3,2,1,0:T(8,128)S(1)}, u32[]{:S(2)}, u32[]{:S(2)}) collective-permute-start(f32[2,8,64,128]{3,2,1,0:T(8,128)S(1)} %turn.17.refs_2_), channel_id=1, source_target_pairs={{0,1},{1,2},{2,3},{3,4},{4,5},{5,6},{6,7},{7,8},{8,9},{9,10},{10,1... | collective-permute-start | bytes 1572872 | tf_op jit(solution)/shard_map/ppermute | solution.py:25
  137.5 0.6 mix.10
  138.1 1.6 advance.21
  139.7 0.6 mix.11
  140.3 1.6 advance.22
  141.9 0.6 mix.12
  142.5 1.7 collective-permute-done.25.refs_4_
  144.2 1.8 %advance.23._ = f32[96,2,64,128]{3,2,1,0:T(8,128)S(1)} custom-call(bf16[768,256]{1,0:T(8,128)(2,1)S(1)} %fusion.8.refs_0_, f32[96,16,128]{2,1,0:T(8,128)S(1)} %bitcast.26, f32[2,8,64,128]{3,2,1,0:T(8,128)S(1)} %turn.17.refs_2_, f32[2,8,64,128]{3,2,1,0:T(8,128)S(1)} %collective-permute-done.24.refs_3_, ...), custom_call_target="tpu_custom_call", output_to_operand_aliasing={{}: (9, {})} | custom-call | flops 786432000 | bytes 2097152 | tf_op jit(solution)/shard_map/advance/pallas_call | solution.py:417
  146.0 0.7 mix.13
  146.8 8.6 %collective-permute-start.30 = (f32[64,64]{1,0:T(8,128)S(1)}, f32[64,64]{1,0:T(8,128)S(1)}, u32[]{:S(2)}, u32[]{:S(2)}) collective-permute-start(f32[64,64]{1,0:T(8,128)S(1)} %slice_add_fusion.1), channel_id=1, source_target_pairs={{0,1},{1,0},{2,3},{3,2},{4,5},{5,4},{6,7},{7,6},{8,9},{9,8},{10,11... | collective-permute-start | bytes 49160 | tf_op jit(solution)/shard_map/ppermute | solution.py:29
  155.3 0.9 collective-permute-done.30
  156.3 0.2 collective-permute-start.31
  156.5 3.7 %collective-permute-done.31 = f32[64,64]{1,0:T(8,128)S(1)} collective-permute-done((f32[64,64]{1,0:T(8,128)S(1)}, f32[64,64]{1,0:T(8,128)S(1)}, u32[]{:S(2)}, u32[]{:S(2)}) %collective-permute-start.31) | collective-permute-done | bytes 16416 | tf_op jit(solution)/shard_map/ppermute | solution.py:29
  160.3 3.9 %collective-permute-done.32 = f32[64,64]{1,0:T(8,128)S(1)} collective-permute-done((f32[64,64]{1,0:T(8,128)S(1)}, f32[64,64]{1,0:T(8,128)S(1)}, u32[]{:S(2)}, u32[]{:S(2)}) %collective-permute-start.32) | collective-permute-done | bytes 16416 | tf_op jit(solution)/shard_map/ppermute | solution.py:29
  164.2 0.4 collective-permute-start.33
  164.6 4.4 %collective-permute-done.33 = f32[64,64]{1,0:T(8,128)S(1)} collective-permute-done((f32[64,64]{1,0:T(8,128)S(1)}, f32[64,64]{1,0:T(8,128)S(1)}, u32[]{:S(2)}, u32[]{:S(2)}) %collective-permute-start.33) | collective-permute-done | bytes 16416 | tf_op jit(solution)/shard_map/ppermute | solution.py:29
  169.0 5.9 %factor.3 = (bf16[64,384]{1,0:T(8,128)(2,1)S(1)}, f32[1,64]{1,0:T(1,128)}) custom-call(f32[64,64]{1,0:T(8,128)S(1)} %add.94.refs_0_, f32[1,64]{1,0:T(1,128)S(1)} %get-tuple-element.116.refs_1_), custom_call_target="tpu_custom_call" | custom-call | tf_op jit(solution)/shard_map/factor/pallas_call | solution.py:211
  174.9 4.3 %finish.1 = f32[64,2,96,128]{3,2,1,0:T(8,128)} custom-call(bf16[64,384]{1,0:T(8,128)(2,1)S(1)} %get-tuple-element.117.inverse_ref, f32[96,2,64,128]{3,2,1,0:T(8,128)S(1)} %get-tuple-element.118.partial_ref), custom_call_target="tpu_custom_call" | custom-call | tf_op jit(solution)/shard_map/finish/pallas_call | solution.py:489
  (72 shorter events, 2.5 us)
Async XLA Ops:
  0.6 2.8 %copy-start = (f32[64,2,96,128]{3,2,1,0:T(8,128)S(1)}, f32[64,2,96,128]{3,2,1,0:T(8,128)}, u32[]{:S(2)}) copy-start(f32[64,2,96,128]{3,2,1,0:T(8,128)} %vectors_ref.25) | copy-start | bytes 18874372
  3.4 5.8 %copy-start.2 = (f32[2,96,128]{2,1,0:T(8,128)S(1)}, f32[2,96,128]{2,1,0:T(8,128)}, u32[]{:S(2)}) copy-start(f32[2,96,128]{2,1,0:T(8,128)} %param.7) | copy-start | bytes 294916
  3.4 5.8 %copy-start.3 = (f32[2,96,128]{2,1,0:T(8,128)S(1)}, f32[2,96,128]{2,1,0:T(8,128)}, u32[]{:S(2)}) copy-start(f32[2,96,128]{2,1,0:T(8,128)} %param.6) | copy-start | bytes 294916
  3.4 5.8 %copy-start.4 = (f32[2,96,128]{2,1,0:T(8,128)S(1)}, f32[2,96,128]{2,1,0:T(8,128)}, u32[]{:S(2)}) copy-start(f32[2,96,128]{2,1,0:T(8,128)} %param.5) | copy-start | bytes 294916
  3.4 10.4 %copy-start.1 = (f32[64,2,96,128]{3,2,1,0:T(8,128)S(1)}, f32[64,2,96,128]{3,2,1,0:T(8,128)}, u32[]{:S(2)}) copy-start(f32[64,2,96,128]{3,2,1,0:T(8,128)} %vectors_ref.25) | copy-start | bytes 18874372
  3.7 27.6 %collective-permute-start.3 = (f32[2,8,64,128]{3,2,1,0:T(8,128)S(1)}, f32[2,8,64,128]{3,2,1,0:T(8,128)S(1)}, u32[]{:S(2)}, u32[]{:S(2)}) collective-permute-start(f32[2,8,64,128]{3,2,1,0:T(8,128)S(1)} %turn.12.refs_2_.refs_5_), channel_id=1, source_target_pairs={{0,1},{1,2},{2,3},{3,4},{4,5},{5,6},{6,7},{7,8},{8,9},{9,10},{10,1... | collective-permute-start | bytes 1572872 | tf_op jit(solution)/shard_map/ppermute | solution.py:25
  4.2 27.6 %collective-permute-start.4 = (f32[2,8,64,128]{3,2,1,0:T(8,128)S(1)}, f32[2,8,64,128]{3,2,1,0:T(8,128)S(1)}, u32[]{:S(2)}, u32[]{:S(2)}) collective-permute-start(f32[2,8,64,128]{3,2,1,0:T(8,128)S(1)} %turn.12.refs_2_.refs_5_), channel_id=1, source_target_pairs={{0,15},{1,0},{2,1},{3,2},{4,3},{5,4},{6,5},{7,6},{8,7},{9,8},{10,9... | collective-permute-start | bytes 1572872 | tf_op jit(solution)/shard_map/ppermute | solution.py:25
  9.3 16.6 %collective-permute-start.1 = (f32[1,3,96,128]{3,2,0,1:T(8,128)S(1)}, f32[1,3,96,128]{3,2,0,1:T(8,128)S(1)}, u32[]{:S(2)}, u32[]{:S(2)}) collective-permute-start(f32[1,3,96,128]{3,2,0,1:T(8,128)S(1)} %get-tuple-element.126), channel_id=1, source_target_pairs={{0,1},{1,2},{2,3},{3,4},{4,5},{5,6},{6,7},{7,8},{8,9},{9,10},{10,1... | collective-permute-start | bytes 442376 | tf_op jit(solution)/shard_map/ppermute | solution.py:25
  9.4 21.1 %collective-permute-start.2 = (f32[1,3,96,128]{3,2,0,1:T(8,128)S(1)}, f32[1,3,96,128]{3,2,0,1:T(8,128)S(1)}, u32[]{:S(2)}, u32[]{:S(2)}) collective-permute-start(f32[1,3,96,128]{3,2,0,1:T(8,128)S(1)} %get-tuple-element.127), channel_id=1, source_target_pairs={{0,15},{1,0},{2,1},{3,2},{4,3},{5,4},{6,5},{7,6},{8,7},{9,8},{10,9... | collective-permute-start | bytes 442376 | tf_op jit(solution)/shard_map/ppermute | solution.py:25
  21.9 4.0 %collective-permute-start = (f32[64,64]{1,0:T(8,128)S(1)}, f32[64,64]{1,0:T(8,128)S(1)}, u32[]{:S(2)}, u32[]{:S(2)}) collective-permute-start(f32[64,64]{1,0:T(8,128)S(1)} %gram.1), channel_id=1, source_target_pairs={{0,2},{1,3},{2,0},{3,1},{4,6},{5,7},{6,4},{7,5},{8,10},{9,11},{10,... | collective-permute-start | bytes 49160 | tf_op jit(solution)/shard_map/ppermute | solution.py:29
  25.9 11.4 %collective-permute-start.6 = (f32[2,8,64,128]{3,2,1,0:T(8,128)S(1)}, f32[2,8,64,128]{3,2,1,0:T(8,128)S(1)}, u32[]{:S(2)}, u32[]{:S(2)}) collective-permute-start(f32[2,8,64,128]{3,2,1,0:T(8,128)S(1)} %turn.13.refs_2_.refs_5_), channel_id=1, source_target_pairs={{0,1},{1,2},{2,3},{3,4},{4,5},{5,6},{6,7},{7,8},{8,9},{9,10},{10,1... | collective-permute-start | bytes 1572872 | tf_op jit(solution)/shard_map/ppermute | solution.py:25
  25.9 12.9 %collective-permute-start.7 = (f32[2,8,64,128]{3,2,1,0:T(8,128)S(1)}, f32[2,8,64,128]{3,2,1,0:T(8,128)S(1)}, u32[]{:S(2)}, u32[]{:S(2)}) collective-permute-start(f32[2,8,64,128]{3,2,1,0:T(8,128)S(1)} %turn.13.refs_2_.refs_5_), channel_id=1, source_target_pairs={{0,15},{1,0},{2,1},{3,2},{4,3},{5,4},{6,5},{7,6},{8,7},{9,8},{10,9... | collective-permute-start | bytes 1572872 | tf_op jit(solution)/shard_map/ppermute | solution.py:25
  30.4 25.6 %collective-permute-start.10 = (f32[2,8,64,128]{3,2,1,0:T(8,128)S(1)}, f32[2,8,64,128]{3,2,1,0:T(8,128)S(1)}, u32[]{:S(2)}, u32[]{:S(2)}) collective-permute-start(f32[2,8,64,128]{3,2,1,0:T(8,128)S(1)} %turn.14.refs_2_.refs_5_), channel_id=1, source_target_pairs={{0,15},{1,0},{2,1},{3,2},{4,3},{5,4},{6,5},{7,6},{8,7},{9,8},{10,9... | collective-permute-start | bytes 1572872 | tf_op jit(solution)/shard_map/ppermute | solution.py:25
  31.2 24.8 %collective-permute-start.9 = (f32[2,8,64,128]{3,2,1,0:T(8,128)S(1)}, f32[2,8,64,128]{3,2,1,0:T(8,128)S(1)}, u32[]{:S(2)}, u32[]{:S(2)}) collective-permute-start(f32[2,8,64,128]{3,2,1,0:T(8,128)S(1)} %turn.14.refs_2_.refs_5_), channel_id=1, source_target_pairs={{0,1},{1,2},{2,3},{3,4},{4,5},{5,6},{6,7},{7,8},{8,9},{9,10},{10,1... | collective-permute-start | bytes 1572872 | tf_op jit(solution)/shard_map/ppermute | solution.py:25
  33.1 1.3 collective-permute-start.5
  34.4 33.8 %collective-permute-start.14 = (f32[2,8,64,128]{3,2,1,0:T(8,128)S(1)}, f32[2,8,64,128]{3,2,1,0:T(8,128)S(1)}, u32[]{:S(2)}, u32[]{:S(2)}) collective-permute-start(f32[2,8,64,128]{3,2,1,0:T(8,128)S(1)} %turn.16.refs_2_.refs_5_), channel_id=1, source_target_pairs={{0,1},{1,2},{2,3},{3,4},{4,5},{5,6},{6,7},{7,8},{8,9},{9,10},{10,1... | collective-permute-start | bytes 1572872 | tf_op jit(solution)/shard_map/ppermute | solution.py:25
  37.3 33.3 %collective-permute-start.15 = (f32[2,8,64,128]{3,2,1,0:T(8,128)S(1)}, f32[2,8,64,128]{3,2,1,0:T(8,128)S(1)}, u32[]{:S(2)}, u32[]{:S(2)}) collective-permute-start(f32[2,8,64,128]{3,2,1,0:T(8,128)S(1)} %turn.16.refs_2_.refs_5_), channel_id=1, source_target_pairs={{0,15},{1,0},{2,1},{3,2},{4,3},{5,4},{6,5},{7,6},{8,7},{9,8},{10,9... | collective-permute-start | bytes 1572872 | tf_op jit(solution)/shard_map/ppermute | solution.py:25
  40.5 8.3 %collective-permute-start.8 = (f32[64,64]{1,0:T(8,128)S(1)}, f32[64,64]{1,0:T(8,128)S(1)}, u32[]{:S(2)}, u32[]{:S(2)}) collective-permute-start(f32[64,64]{1,0:T(8,128)S(1)} %add.85), channel_id=1, source_target_pairs={{0,4},{1,5},{2,6},{3,7},{4,0},{5,1},{6,2},{7,3},{8,12},{9,13},{10,... | collective-permute-start | bytes 49160 | tf_op jit(solution)/shard_map/ppermute | solution.py:29
  48.7 24.2 %collective-permute-start.12 = (f32[2,8,64,128]{3,2,1,0:T(8,128)S(1)}, f32[2,8,64,128]{3,2,1,0:T(8,128)S(1)}, u32[]{:S(2)}, u32[]{:S(2)}) collective-permute-start(f32[2,8,64,128]{3,2,1,0:T(8,128)S(1)} %turn.15.refs_2_.refs_5_), channel_id=1, source_target_pairs={{0,1},{1,2},{2,3},{3,4},{4,5},{5,6},{6,7},{7,8},{8,9},{9,10},{10,1... | collective-permute-start | bytes 1572872 | tf_op jit(solution)/shard_map/ppermute | solution.py:25
  56.0 21.5 %collective-permute-start.13 = (f32[2,8,64,128]{3,2,1,0:T(8,128)S(1)}, f32[2,8,64,128]{3,2,1,0:T(8,128)S(1)}, u32[]{:S(2)}, u32[]{:S(2)}) collective-permute-start(f32[2,8,64,128]{3,2,1,0:T(8,128)S(1)} %turn.15.refs_2_.refs_5_), channel_id=1, source_target_pairs={{0,15},{1,0},{2,1},{3,2},{4,3},{5,4},{6,5},{7,6},{8,7},{9,8},{10,9... | collective-permute-start | bytes 1572872 | tf_op jit(solution)/shard_map/ppermute | solution.py:25
  57.7 8.2 %collective-permute-start.11 = (f32[64,64]{1,0:T(8,128)S(1)}, f32[64,64]{1,0:T(8,128)S(1)}, u32[]{:S(2)}, u32[]{:S(2)}) collective-permute-start(f32[64,64]{1,0:T(8,128)S(1)} %add.86), channel_id=1, source_target_pairs={{0,8},{1,9},{2,10},{3,11},{4,12},{5,13},{6,14},{7,15},{8,0},{9,1},... | collective-permute-start | bytes 49160 | tf_op jit(solution)/shard_map/ppermute | solution.py:29
  65.9 26.4 %collective-permute-start.16 = (f32[2,8,64,128]{3,2,1,0:T(8,128)S(1)}, f32[2,8,64,128]{3,2,1,0:T(8,128)S(1)}, u32[]{:S(2)}, u32[]{:S(2)}) collective-permute-start(f32[2,8,64,128]{3,2,1,0:T(8,128)S(1)} %turn.19.refs_2_.refs_5_), channel_id=1, source_target_pairs={{0,1},{1,2},{2,3},{3,4},{4,5},{5,6},{6,7},{7,8},{8,9},{9,10},{10,1... | collective-permute-start | bytes 1572872 | tf_op jit(solution)/shard_map/ppermute | solution.py:25
  68.1 24.1 %collective-permute-start.17 = (f32[2,8,64,128]{3,2,1,0:T(8,128)S(1)}, f32[2,8,64,128]{3,2,1,0:T(8,128)S(1)}, u32[]{:S(2)}, u32[]{:S(2)}) collective-permute-start(f32[2,8,64,128]{3,2,1,0:T(8,128)S(1)} %turn.19.refs_2_.refs_5_), channel_id=1, source_target_pairs={{0,15},{1,0},{2,1},{3,2},{4,3},{5,4},{6,5},{7,6},{8,7},{9,8},{10,9... | collective-permute-start | bytes 1572872 | tf_op jit(solution)/shard_map/ppermute | solution.py:25
  72.2 29.5 %collective-permute-start.22 = (f32[2,8,64,128]{3,2,1,0:T(8,128)S(1)}, f32[2,8,64,128]{3,2,1,0:T(8,128)S(1)}, u32[]{:S(2)}, u32[]{:S(2)}) collective-permute-start(f32[2,8,64,128]{3,2,1,0:T(8,128)S(1)} %turn.21.refs_2_.refs_5_), channel_id=1, source_target_pairs={{0,1},{1,2},{2,3},{3,4},{4,5},{5,6},{6,7},{7,8},{8,9},{9,10},{10,1... | collective-permute-start | bytes 1572872 | tf_op jit(solution)/shard_map/ppermute | solution.py:25
  72.9 29.0 %collective-permute-start.23 = (f32[2,8,64,128]{3,2,1,0:T(8,128)S(1)}, f32[2,8,64,128]{3,2,1,0:T(8,128)S(1)}, u32[]{:S(2)}, u32[]{:S(2)}) collective-permute-start(f32[2,8,64,128]{3,2,1,0:T(8,128)S(1)} %turn.21.refs_2_.refs_5_), channel_id=1, source_target_pairs={{0,15},{1,0},{2,1},{3,2},{4,3},{5,4},{6,5},{7,6},{8,7},{9,8},{10,9... | collective-permute-start | bytes 1572872 | tf_op jit(solution)/shard_map/ppermute | solution.py:25
  84.4 25.4 %collective-permute-start.20 = (f32[2,8,64,128]{3,2,1,0:T(8,128)S(1)}, f32[2,8,64,128]{3,2,1,0:T(8,128)S(1)}, u32[]{:S(2)}, u32[]{:S(2)}) collective-permute-start(f32[2,8,64,128]{3,2,1,0:T(8,128)S(1)} %turn.20.refs_2_.refs_5_), channel_id=1, source_target_pairs={{0,1},{1,2},{2,3},{3,4},{4,5},{5,6},{6,7},{7,8},{8,9},{9,10},{10,1... | collective-permute-start | bytes 1572872 | tf_op jit(solution)/shard_map/ppermute | solution.py:25
  92.3 18.3 %collective-permute-start.21 = (f32[2,8,64,128]{3,2,1,0:T(8,128)S(1)}, f32[2,8,64,128]{3,2,1,0:T(8,128)S(1)}, u32[]{:S(2)}, u32[]{:S(2)}) collective-permute-start(f32[2,8,64,128]{3,2,1,0:T(8,128)S(1)} %turn.20.refs_2_.refs_5_), channel_id=1, source_target_pairs={{0,15},{1,0},{2,1},{3,2},{4,3},{5,4},{6,5},{7,6},{8,7},{9,8},{10,9... | collective-permute-start | bytes 1572872 | tf_op jit(solution)/shard_map/ppermute | solution.py:25
  93.9 26.8 %collective-permute-start.18 = (f32[2,8,64,128]{3,2,1,0:T(8,128)S(1)}, f32[2,8,64,128]{3,2,1,0:T(8,128)S(1)}, u32[]{:S(2)}, u32[]{:S(2)}) collective-permute-start(f32[2,8,64,128]{3,2,1,0:T(8,128)S(1)} %turn.18.refs_2_.refs_5_), channel_id=1, source_target_pairs={{0,1},{1,2},{2,3},{3,4},{4,5},{5,6},{6,7},{7,8},{8,9},{9,10},{10,1... | collective-permute-start | bytes 1572872 | tf_op jit(solution)/shard_map/ppermute | solution.py:25
  101.7 19.5 %collective-permute-start.19 = (f32[2,8,64,128]{3,2,1,0:T(8,128)S(1)}, f32[2,8,64,128]{3,2,1,0:T(8,128)S(1)}, u32[]{:S(2)}, u32[]{:S(2)}) collective-permute-start(f32[2,8,64,128]{3,2,1,0:T(8,128)S(1)} %turn.18.refs_2_.refs_5_), channel_id=1, source_target_pairs={{0,15},{1,0},{2,1},{3,2},{4,3},{5,4},{6,5},{7,6},{8,7},{9,8},{10,9... | collective-permute-start | bytes 1572872 | tf_op jit(solution)/shard_map/ppermute | solution.py:25
  103.6 33.9 %collective-permute-start.28 = (f32[2,8,64,128]{3,2,1,0:T(8,128)S(1)}, f32[2,8,64,128]{3,2,1,0:T(8,128)S(1)}, u32[]{:S(2)}, u32[]{:S(2)}) collective-permute-start(f32[2,8,64,128]{3,2,1,0:T(8,128)S(1)} %turn.23.refs_2_.refs_5_), channel_id=1, source_target_pairs={{0,1},{1,2},{2,3},{3,4},{4,5},{5,6},{6,7},{7,8},{8,9},{9,10},{10,1... | collective-permute-start | bytes 1572872 | tf_op jit(solution)/shard_map/ppermute | solution.py:25
  109.9 28.2 %collective-permute-start.29 = (f32[2,8,64,128]{3,2,1,0:T(8,128)S(1)}, f32[2,8,64,128]{3,2,1,0:T(8,128)S(1)}, u32[]{:S(2)}, u32[]{:S(2)}) collective-permute-start(f32[2,8,64,128]{3,2,1,0:T(8,128)S(1)} %turn.23.refs_2_.refs_5_), channel_id=1, source_target_pairs={{0,15},{1,0},{2,1},{3,2},{4,3},{5,4},{6,5},{7,6},{8,7},{9,8},{10,9... | collective-permute-start | bytes 1572872 | tf_op jit(solution)/shard_map/ppermute | solution.py:25
  112.2 28.1 %collective-permute-start.26 = (f32[2,8,64,128]{3,2,1,0:T(8,128)S(1)}, f32[2,8,64,128]{3,2,1,0:T(8,128)S(1)}, u32[]{:S(2)}, u32[]{:S(2)}) collective-permute-start(f32[2,8,64,128]{3,2,1,0:T(8,128)S(1)} %turn.22.refs_2_.refs_5_), channel_id=1, source_target_pairs={{0,1},{1,2},{2,3},{3,4},{4,5},{5,6},{6,7},{7,8},{8,9},{9,10},{10,1... | collective-permute-start | bytes 1572872 | tf_op jit(solution)/shard_map/ppermute | solution.py:25
  120.6 19.7 %collective-permute-start.27 = (f32[2,8,64,128]{3,2,1,0:T(8,128)S(1)}, f32[2,8,64,128]{3,2,1,0:T(8,128)S(1)}, u32[]{:S(2)}, u32[]{:S(2)}) collective-permute-start(f32[2,8,64,128]{3,2,1,0:T(8,128)S(1)} %turn.22.refs_2_.refs_5_), channel_id=1, source_target_pairs={{0,15},{1,0},{2,1},{3,2},{4,3},{5,4},{6,5},{7,6},{8,7},{9,8},{10,9... | collective-permute-start | bytes 1572872 | tf_op jit(solution)/shard_map/ppermute | solution.py:25
  122.8 19.7 %collective-permute-start.24 = (f32[2,8,64,128]{3,2,1,0:T(8,128)S(1)}, f32[2,8,64,128]{3,2,1,0:T(8,128)S(1)}, u32[]{:S(2)}, u32[]{:S(2)}) collective-permute-start(f32[2,8,64,128]{3,2,1,0:T(8,128)S(1)} %turn.17.refs_2_), channel_id=1, source_target_pairs={{0,1},{1,2},{2,3},{3,4},{4,5},{5,6},{6,7},{7,8},{8,9},{9,10},{10,1... | collective-permute-start | bytes 1572872 | tf_op jit(solution)/shard_map/ppermute | solution.py:25
  137.5 6.7 %collective-permute-start.25 = (f32[2,8,64,128]{3,2,1,0:T(8,128)S(1)}, f32[2,8,64,128]{3,2,1,0:T(8,128)S(1)}, u32[]{:S(2)}, u32[]{:S(2)}) collective-permute-start(f32[2,8,64,128]{3,2,1,0:T(8,128)S(1)} %turn.17.refs_2_), channel_id=1, source_target_pairs={{0,15},{1,0},{2,1},{3,2},{4,3},{5,4},{6,5},{7,6},{8,7},{9,8},{10,9... | collective-permute-start | bytes 1572872 | tf_op jit(solution)/shard_map/ppermute | solution.py:25
  146.8 9.4 %collective-permute-start.30 = (f32[64,64]{1,0:T(8,128)S(1)}, f32[64,64]{1,0:T(8,128)S(1)}, u32[]{:S(2)}, u32[]{:S(2)}) collective-permute-start(f32[64,64]{1,0:T(8,128)S(1)} %slice_add_fusion.1), channel_id=1, source_target_pairs={{0,1},{1,0},{2,3},{3,2},{4,5},{5,4},{6,7},{7,6},{8,9},{9,8},{10,11... | collective-permute-start | bytes 49160 | tf_op jit(solution)/shard_map/ppermute | solution.py:29
  156.3 4.0 %collective-permute-start.31 = (f32[64,64]{1,0:T(8,128)S(1)}, f32[64,64]{1,0:T(8,128)S(1)}, u32[]{:S(2)}, u32[]{:S(2)}) collective-permute-start(f32[64,64]{1,0:T(8,128)S(1)} %fusion.12), channel_id=1, source_target_pairs={{0,2},{1,3},{2,0},{3,1},{4,6},{5,7},{6,4},{7,5},{8,10},{9,11},{10,... | collective-permute-start | bytes 49160 | tf_op jit(solution)/shard_map/ppermute | solution.py:29
  160.3 3.9 %collective-permute-start.32 = (f32[64,64]{1,0:T(8,128)S(1)}, f32[64,64]{1,0:T(8,128)S(1)}, u32[]{:S(2)}, u32[]{:S(2)}) collective-permute-start(f32[64,64]{1,0:T(8,128)S(1)} %add.92), channel_id=1, source_target_pairs={{0,4},{1,5},{2,6},{3,7},{4,0},{5,1},{6,2},{7,3},{8,12},{9,13},{10,... | collective-permute-start | bytes 49160 | tf_op jit(solution)/shard_map/ppermute | solution.py:29
  164.2 4.8 %collective-permute-start.33 = (f32[64,64]{1,0:T(8,128)S(1)}, f32[64,64]{1,0:T(8,128)S(1)}, u32[]{:S(2)}, u32[]{:S(2)}) collective-permute-start(f32[64,64]{1,0:T(8,128)S(1)} %add.93), channel_id=1, source_target_pairs={{0,8},{1,9},{2,10},{3,11},{4,12},{5,13},{6,14},{7,15},{8,0},{9,1},... | collective-permute-start | bytes 49160 | tf_op jit(solution)/shard_map/ppermute | solution.py:29
where the time goes:
time: 180 us; the launch traced here: 179 us
  starting transfers between devices  85.4 us (47%)
  Pallas kernels  52.8 us (29%)
  waiting for transfers between devices  35.6 us (20%)
  local copies, waits for them, and re-layouts  3.34 us (2%)
    ppermute x26, starting transfers between devices, shift(): lax.ppermute(block, axis, [(i, (i + step) % count) for i in range(count)])  74.4 us
    ppermute x8, waiting for transfers between devices, exchange(): lax.ppermute(value, axis, [(i, i ^ hop) for i in range(lax.axis_size(axis...  31.1 us
    pallas_call x12, Pallas kernels, advance(): pl.pallas_call(functools.partial(advance_kernel, first, last, base - 2),...  19 us
    pallas_call x2, Pallas kernels, factor(): pl.pallas_call(functools.partial(factor_kernel, 1.0 / total), out_shape=[...  11.2 us
    ppermute x8, starting transfers between devices, exchange(): lax.ppermute(value, axis, [(i, i ^ hop) for i in range(lax.axis_size(axis...  11.1 us
    pallas_call x1, Pallas kernels, gram_of(): pl.pallas_call(gram_kernel, in_specs=[pl.BlockSpec(memory_space=pltpu.HBM...  8.12 us
    pallas_call x7, Pallas kernels, mix(): pl.pallas_call(functools.partial(mix_kernel, start, stop), in_specs=[memo...  7.23 us
    ppermute x26, waiting for transfers between devices, shift(): lax.ppermute(block, axis, [(i, (i + step) % count) for i in range(count)])  4.53 us
  transfers between devices with their start and end apart: 34, of which 10 were waited for; matrix products, arithmetic and copies ran while one was open for 1% of the time, Pallas kernels for 22%

commit v1 on v0

--- a/solution.py
+++ b/solution.py
@@ -13,6 +13,7 @@
 BF16 = jnp.bfloat16
 ROWS = 8
 UNROLL = 8
+PIVOTS = 4
 FUSED = 5
 HOP_EVERY = 1
 STEP = 0.3
@@ -123,7 +124,7 @@
     )(vectors)
 
 
-def gram_kernel(vectors_ref, gram_ref, slots, sems):
+def gram_kernel(vectors_ref, gram_ref, slots, sems, acc):
     count, planes, height, points = vectors_ref.shape
     steps = height // ROWS
 
@@ -134,7 +135,7 @@
             sems.at[step % 2],
         )
 
-    gram_ref[...] = jnp.zeros_like(gram_ref)
+    acc[...] = jnp.zeros_like(acc)
     fetch(0).start()
 
     def body(step, carry):
@@ -144,7 +145,7 @@
 
         fetch(step).wait()
         flat = slots.at[step % 2].reshape(count * planes * ROWS, points)
-        total = jnp.zeros((count, count), F32)
+        total = jnp.zeros(acc.shape, F32)
         for row in range(ROWS):
             both = jnp.concatenate(
                 [
@@ -153,11 +154,18 @@
                 ],
                 axis=1,
             )
-            total += dot_nt(both, both, HIGH)
-        gram_ref[...] += total
+            split = jnp.concatenate(pieces(both), axis=0)
+            total += dot_nt(split, split)
+        acc[...] += total
         return carry
 
     lax.fori_loop(0, steps, body, 0)
+    parts = [acc[k * count : (k + 1) * count, :] for k in range(3)]
+    gram_ref[...] = (
+        parts[0][:, :count]
+        + (parts[0][:, count : 2 * count] + parts[1][:, :count])
+        + (parts[1][:, count : 2 * count] + parts[0][:, 2 * count :] + parts[2][:, :count])
+    )
 
 
 def gram_of(vectors):
@@ -170,6 +178,7 @@
         scratch_shapes=[
             pltpu.VMEM((2, count, planes, ROWS, points), F32),
             pltpu.SemaphoreType.DMA((2,)),
+            pltpu.VMEM((3 * count, 3 * count), F32),
         ],
         compiler_params=pltpu.CompilerParams(vmem_limit_bytes=16 * 1024 * 1024),
         cost_estimate=pl.CostEstimate(
@@ -189,15 +198,39 @@
     gram = gram_ref[...] * scale
     work = jnp.concatenate([gram, jnp.where(rows == lanes, 1.0, 0.0).astype(F32)], axis=1)
     blocks = [work[i : i + tile] for i in range(0, count, tile)]
-    for j in range(count):
+    for j in range(0, count, PIVOTS):
         here, inner = divmod(j, tile)
-        row = blocks[here][inner : inner + 1]
-        root = lax.rsqrt(row[:, j : j + 1])
-        scaled = row * root
-        upper_ref[j : j + 1, :] = scaled
-        row_all = jnp.broadcast_to(scaled, (tile, 2 * count))
-        for b in range(here, len(blocks)):
-            blocks[b] = blocks[b] - (blocks[b][:, j : j + 1] * root) * row_all
+        spread = [
+            [
+                jnp.broadcast_to(blocks[b][:, j + q : j + q + 1], (tile, 2 * count))
+                for q in range(PIVOTS)
+            ]
+            for b in range(here, len(blocks))
+        ]
+        lower = {}
+        roots, scaled = [], []
+        for q in range(PIVOTS):
+            pivot = spread[0][q][inner + q : inner + q + 1]
+            row = blocks[here][inner + q : inner + q + 1]
+            for t in range(q):
+                pivot = pivot - lower[q, t] * lower[q, t]
+                row = row - lower[q, t] * scaled[t]
+            roots.append(lax.rsqrt(pivot))
+            scaled.append(row * roots[q])
+            upper_ref[j + q : j + q + 1, :] = scaled[q]
+            for p in range(q + 1, PIVOTS):
+                entry = spread[0][q][inner + p : inner + p + 1]
+                for t in range(q):
+                    entry = entry - lower[p, t] * lower[q, t]
+                lower[p, q] = entry * roots[q]
+        for k, b in enumerate(range(here, len(blocks))):
+            columns = []
+            for q in range(PIVOTS):
+                column = spread[k][q]
+                for t in range(q):
+                    column = column - columns[t] * lower[q, t]
+                columns.append(column * roots[q])
+                blocks[b] = blocks[b] - columns[q] * scaled[q]
     upper = upper_ref[...]
     left_ref[...] = split_six_left(upper[:, count:])
     diagonal = jnp.where(rows == lanes, upper[:, :count], 0.0)
@@ -557,7 +590,7 @@
     coefs = coefficient_rows(stream_speed, span_speed, damping)
     send()
     send()
-    gram = gram_of(vectors)
+    gram = gram_of(gated(vectors, own[1]))
     send(gram)
     hops = [1 << k for k in range((members - 1).bit_length())]
     gram = gram + exchange(gram, "gx", hops.pop(len(hops) > 1))

time: 180 us -> 175 us (0.972)
  Pallas kernels: 52.8 us -> 44.6 us
  starting transfers between devices: 85.4 us -> 89.8 us
    pallas_call x2, Pallas kernels: 11.2 us -> 4.64 us  [factor(): pl.pallas_call(functools.partial(factor_kernel, 1.0 / total), out_shape=[...]
    ppermute x8, starting transfers between devices: 11.1 us -> 16.1 us  [exchange(): lax.ppermute(value, axis, [(i, i ^ hop) for i in range(lax.axis_size(axis...]
  transfers between devices with their start and end apart: 34 -> 34, of which waited for: 10 -> 10; matrix products, arithmetic and copies ran while one was open for 1% -> 1% of each run, Pallas kernels for 22% -> 20%
where the time goes in v1:
time: 175 us
  starting transfers between devices  89.8 us (51%)
  Pallas kernels  44.6 us (25%)
  waiting for transfers between devices  35.3 us (20%)
  local copies, waits for them, and re-layouts  3.34 us (2%)
    ppermute x26, starting transfers between devices, shift(): lax.ppermute(block, axis, [(i, (i + step) % count) for i in range(count)])  73.7 us
    ppermute x8, waiting for transfers between devices, exchange(): lax.ppermute(value, axis, [(i, i ^ hop) for i in range(lax.axis_size(axis...  30.5 us
    pallas_call x12, Pallas kernels, advance(): pl.pallas_call(functools.partial(advance_kernel, first, last, base - 2),...  19 us
    ppermute x8, starting transfers between devices, exchange(): lax.ppermute(value, axis, [(i, i ^ hop) for i in range(lax.axis_size(axis...  16.1 us
    pallas_call x7, Pallas kernels, mix(): pl.pallas_call(functools.partial(mix_kernel, start, stop), in_specs=[memo...  7.21 us
    pallas_call x1, Pallas kernels, gram_of(): pl.pallas_call(gram_kernel, in_specs=[pl.BlockSpec(memory_space=pltpu.HBM...  6.57 us
    ppermute x26, waiting for transfers between devices, shift(): lax.ppermute(block, axis, [(i, (i + step) % count) for i in range(count)])  4.8 us
    pallas_call x2, Pallas kernels, factor(): pl.pallas_call(functools.partial(factor_kernel, 1.0 / total), out_shape=[...  4.64 us
  transfers between devices with their start and end apart: 34, of which 10 were waited for; matrix products, arithmetic and copies ran while one was open for 1% of the time, Pallas kernels for 20%

profile of v1, /device:TPU:0, one launch (start us, length us, event | category | flops | bytes accessed | tf_op | source)
XLA Modules:
  0.0 175.2 jit_solution(17764959147706586386)
XLA Ops:
  0.6 2.8 %copy-done = f32[64,2,96,128]{3,2,1,0:T(8,128)S(1)} copy-done((f32[64,2,96,128]{3,2,1,0:T(8,128)S(1)}, f32[64,2,96,128]{3,2,1,0:T(8,128)}, u32[]{:S(2)}) %copy-start) | copy-done | bytes 6291480
  3.4 0.2 turn.13.refs_2_.refs_5_
  3.7 0.5 collective-permute-start.3
  4.2 5.1 %collective-permute-start.4 = (f32[2,8,64,128]{3,2,1,0:T(8,128)S(1)}, f32[2,8,64,128]{3,2,1,0:T(8,128)S(1)}, u32[]{:S(2)}, u32[]{:S(2)}) collective-permute-start(f32[2,8,64,128]{3,2,1,0:T(8,128)S(1)} %turn.13.refs_2_.refs_5_), channel_id=1, source_target_pairs={{0,15},{1,0},{2,1},{3,2},{4,3},{5,4},{6,5},{7,6},{8,7},{9,8},{10,9... | collective-permute-start | bytes 1572872 | tf_op jit(solution)/shard_map/ppermute | solution.py:26
  9.4 4.4 %collective-permute-start.2 = (f32[1,3,96,128]{3,2,0,1:T(8,128)S(1)}, f32[1,3,96,128]{3,2,0,1:T(8,128)S(1)}, u32[]{:S(2)}, u32[]{:S(2)}) collective-permute-start(f32[1,3,96,128]{3,2,0,1:T(8,128)S(1)} %get-tuple-element.129), channel_id=1, source_target_pairs={{0,15},{1,0},{2,1},{3,2},{4,3},{5,4},{6,5},{7,6},{8,7},{9,8},{10,9... | collective-permute-start | bytes 442376 | tf_op jit(solution)/shard_map/ppermute | solution.py:26
  13.8 0.2 turn.12.refs_2_.refs_5_
  14.1 6.6 %gram.1 = f32[64,64]{1,0:T(8,128)S(1)} custom-call(f32[64,2,96,128]{3,2,1,0:T(8,128)S(1)} %copy-done.1), custom_call_target="tpu_custom_call" | custom-call | flops 1207959552 | bytes 6291456 | tf_op jit(solution)/shard_map/gram/pallas_call | solution.py:173
  20.7 0.3 multiply_select_fusion
  21.2 0.2 turn.14.refs_2_.refs_5_
  21.4 3.6 %collective-permute-done = f32[64,64]{1,0:T(8,128)S(1)} collective-permute-done((f32[64,64]{1,0:T(8,128)S(1)}, f32[64,64]{1,0:T(8,128)S(1)}, u32[]{:S(2)}, u32[]{:S(2)}) %collective-permute-start) | collective-permute-done | bytes 16416 | tf_op jit(solution)/shard_map/ppermute | solution.py:30
  25.1 4.5 %collective-permute-start.7 = (f32[2,8,64,128]{3,2,1,0:T(8,128)S(1)}, f32[2,8,64,128]{3,2,1,0:T(8,128)S(1)}, u32[]{:S(2)}, u32[]{:S(2)}) collective-permute-start(f32[2,8,64,128]{3,2,1,0:T(8,128)S(1)} %turn.12.refs_2_.refs_5_), channel_id=1, source_target_pairs={{0,15},{1,0},{2,1},{3,2},{4,3},{5,4},{6,5},{7,6},{8,7},{9,8},{10,9... | collective-permute-start | bytes 1572872 | tf_op jit(solution)/shard_map/ppermute | solution.py:26
  29.9 0.5 copy.24
  30.4 0.5 collective-permute-start.9
  30.9 1.3 advance.12
  32.6 0.9 collective-permute-done.5
  33.7 2.8 %collective-permute-done.6.refs_3_.refs_6_ = f32[2,8,64,128]{3,2,1,0:T(8,128)S(1)} collective-permute-done((f32[2,8,64,128]{3,2,1,0:T(8,128)S(1)}, f32[2,8,64,128]{3,2,1,0:T(8,128)S(1)}, u32[]{:S(2)}, u32[]{:S(2)}) %collective-permute-start.6) | collective-permute-done | bytes 524320 | tf_op jit(solution)/shard_map/ppermute | solution.py:26
  36.5 1.5 collective-permute-start.15
  38.0 1.6 advance.13
  39.7 0.2 turn.15.refs_2_.refs_5_
  39.9 8.0 %collective-permute-done.8 = f32[64,64]{1,0:T(8,128)S(1)} collective-permute-done((f32[64,64]{1,0:T(8,128)S(1)}, f32[64,64]{1,0:T(8,128)S(1)}, u32[]{:S(2)}, u32[]{:S(2)}) %collective-permute-start.8) | collective-permute-done | bytes 16416 | tf_op jit(solution)/shard_map/ppermute | solution.py:30
  47.9 6.9 %collective-permute-start.12 = (f32[2,8,64,128]{3,2,1,0:T(8,128)S(1)}, f32[2,8,64,128]{3,2,1,0:T(8,128)S(1)}, u32[]{:S(2)}, u32[]{:S(2)}) collective-permute-start(f32[2,8,64,128]{3,2,1,0:T(8,128)S(1)} %turn.15.refs_2_.refs_5_), channel_id=1, source_target_pairs={{0,1},{1,2},{2,3},{3,4},{4,5},{5,6},{6,7},{7,8},{8,9},{9,10},{10,1... | collective-permute-start | bytes 1572872 | tf_op jit(solution)/shard_map/ppermute | solution.py:26
  54.9 1.0 collective-permute-start.13
  55.8 1.6 advance.14
  57.4 0.8 collective-permute-start.11
  58.2 0.2 turn.19.refs_2_.refs_5_
  58.5 6.3 %collective-permute-done.11 = f32[64,64]{1,0:T(8,128)S(1)} collective-permute-done((f32[64,64]{1,0:T(8,128)S(1)}, f32[64,64]{1,0:T(8,128)S(1)}, u32[]{:S(2)}, u32[]{:S(2)}) %collective-permute-start.11) | collective-permute-done | bytes 16416 | tf_op jit(solution)/shard_map/ppermute | solution.py:30
  64.8 4.4 %collective-permute-start.17 = (f32[2,8,64,128]{3,2,1,0:T(8,128)S(1)}, f32[2,8,64,128]{3,2,1,0:T(8,128)S(1)}, u32[]{:S(2)}, u32[]{:S(2)}) collective-permute-start(f32[2,8,64,128]{3,2,1,0:T(8,128)S(1)} %turn.19.refs_2_.refs_5_), channel_id=1, source_target_pairs={{0,15},{1,0},{2,1},{3,2},{4,3},{5,4},{6,5},{7,6},{8,7},{9,8},{10,9... | collective-permute-start | bytes 1572872 | tf_op jit(solution)/shard_map/ppermute | solution.py:26
  69.5 1.6 advance.15
  71.2 4.4 %collective-permute-start.23 = (f32[2,8,64,128]{3,2,1,0:T(8,128)S(1)}, f32[2,8,64,128]{3,2,1,0:T(8,128)S(1)}, u32[]{:S(2)}, u32[]{:S(2)}) collective-permute-start(f32[2,8,64,128]{3,2,1,0:T(8,128)S(1)} %turn.21.refs_2_.refs_5_), channel_id=1, source_target_pairs={{0,15},{1,0},{2,1},{3,2},{4,3},{5,4},{6,5},{7,6},{8,7},{9,8},{10,9... | collective-permute-start | bytes 1572872 | tf_op jit(solution)/shard_map/ppermute | solution.py:26
  75.9 0.2 turn.18.refs_2_.refs_5_
  76.1 0.2 turn.23.refs_2_.refs_5_
  76.4 1.6 advance.16
  78.0 2.1 %factor.2 = (bf16[64,384]{1,0:T(8,128)(2,1)S(1)}, f32[1,64]{1,0:T(1,128)S(1)}) custom-call(f32[64,64]{1,0:T(8,128)S(1)} %add.87.refs_0_), custom_call_target="tpu_custom_call" | custom-call | tf_op jit(solution)/shard_map/factor/pallas_call | solution.py:244
  80.0 7.8 %collective-permute-start.20 = (f32[2,8,64,128]{3,2,1,0:T(8,128)S(1)}, f32[2,8,64,128]{3,2,1,0:T(8,128)S(1)}, u32[]{:S(2)}, u32[]{:S(2)}) collective-permute-start(f32[2,8,64,128]{3,2,1,0:T(8,128)S(1)} %turn.20.refs_2_.refs_5_), channel_id=1, source_target_pairs={{0,1},{1,2},{2,3},{3,4},{4,5},{5,6},{6,7},{7,8},{8,9},{9,10},{10,1... | collective-permute-start | bytes 1572872 | tf_op jit(solution)/shard_map/ppermute | solution.py:26
  87.8 1.6 advance.17
  89.4 7.6 %collective-permute-start.18 = (f32[2,8,64,128]{3,2,1,0:T(8,128)S(1)}, f32[2,8,64,128]{3,2,1,0:T(8,128)S(1)}, u32[]{:S(2)}, u32[]{:S(2)}) collective-permute-start(f32[2,8,64,128]{3,2,1,0:T(8,128)S(1)} %turn.18.refs_2_.refs_5_), channel_id=1, source_target_pairs={{0,1},{1,2},{2,3},{3,4},{4,5},{5,6},{6,7},{7,8},{8,9},{9,10},{10,1... | collective-permute-start | bytes 1572872 | tf_op jit(solution)/shard_map/ppermute | solution.py:26
  97.0 3.5 %mix.7 = (f32[96,2,64,128]{3,2,1,0:T(8,128)S(1)}, f32[128,128]{1,0:T(8,128)S(1)}) custom-call(bf16[64,384]{1,0:T(8,128)(2,1)S(1)} %get-tuple-element.84.mixer_ref, f32[96,2,64,128]{3,2,1,0:T(8,128)S(1)} %get-tuple-element.91._), custom_call_target="tpu_custom_call", output_to_operand_aliasing={{0}: (1, {})} | custom-call | flops 964689920 | bytes 6029312 | tf_op jit(solution)/shard_map/mix/pallas_call | solution.py:305
  100.6 1.6 advance.18
  102.2 6.0 %collective-permute-start.28 = (f32[2,8,64,128]{3,2,1,0:T(8,128)S(1)}, f32[2,8,64,128]{3,2,1,0:T(8,128)S(1)}, u32[]{:S(2)}, u32[]{:S(2)}) collective-permute-start(f32[2,8,64,128]{3,2,1,0:T(8,128)S(1)} %turn.23.refs_2_.refs_5_), channel_id=1, source_target_pairs={{0,1},{1,2},{2,3},{3,4},{4,5},{5,6},{6,7},{7,8},{8,9},{9,10},{10,1... | collective-permute-start | bytes 1572872 | tf_op jit(solution)/shard_map/ppermute | solution.py:26
  108.5 0.2 turn.17.refs_2_
  108.8 0.6 mix.8
  109.4 1.6 advance.19
  111.0 14.1 %collective-permute-start.26 = (f32[2,8,64,128]{3,2,1,0:T(8,128)S(1)}, f32[2,8,64,128]{3,2,1,0:T(8,128)S(1)}, u32[]{:S(2)}, u32[]{:S(2)}) collective-permute-start(f32[2,8,64,128]{3,2,1,0:T(8,128)S(1)} %turn.22.refs_2_.refs_5_), channel_id=1, source_target_pairs={{0,1},{1,2},{2,3},{3,4},{4,5},{5,6},{6,7},{7,8},{8,9},{9,10},{10,1... | collective-permute-start | bytes 1572872 | tf_op jit(solution)/shard_map/ppermute | solution.py:26
  125.1 0.6 mix.9
  125.7 1.6 advance.20
  127.3 3.4 %collective-permute-start.24 = (f32[2,8,64,128]{3,2,1,0:T(8,128)S(1)}, f32[2,8,64,128]{3,2,1,0:T(8,128)S(1)}, u32[]{:S(2)}, u32[]{:S(2)}) collective-permute-start(f32[2,8,64,128]{3,2,1,0:T(8,128)S(1)} %turn.17.refs_2_), channel_id=1, source_target_pairs={{0,1},{1,2},{2,3},{3,4},{4,5},{5,6},{6,7},{7,8},{8,9},{9,10},{10,1... | collective-permute-start | bytes 1572872 | tf_op jit(solution)/shard_map/ppermute | solution.py:26
  130.7 1.1 collective-permute-start.25
  131.8 0.6 mix.10
  132.4 1.6 advance.21
  134.0 0.6 mix.11
  134.6 1.6 advance.22
  136.2 0.6 mix.12
  136.8 1.9 %collective-permute-done.24.refs_3_ = f32[2,8,64,128]{3,2,1,0:T(8,128)S(1)} collective-permute-done((f32[2,8,64,128]{3,2,1,0:T(8,128)S(1)}, f32[2,8,64,128]{3,2,1,0:T(8,128)S(1)}, u32[]{:S(2)}, u32[]{:S(2)}) %collective-permute-start.24) | collective-permute-done | bytes 524320 | tf_op jit(solution)/shard_map/ppermute | solution.py:26
  138.8 1.8 %advance.23._ = f32[96,2,64,128]{3,2,1,0:T(8,128)S(1)} custom-call(bf16[768,256]{1,0:T(8,128)(2,1)S(1)} %fusion.8.refs_0_, f32[96,16,128]{2,1,0:T(8,128)S(1)} %bitcast.26, f32[2,8,64,128]{3,2,1,0:T(8,128)S(1)} %turn.17.refs_2_, f32[2,8,64,128]{3,2,1,0:T(8,128)S(1)} %collective-permute-done.24.refs_3_, ...), custom_call_target="tpu_custom_call", output_to_operand_aliasing={{}: (9, {})} | custom-call | flops 786432000 | bytes 2097152 | tf_op jit(solution)/shard_map/advance/pallas_call | solution.py:450
  140.6 0.7 mix.13
  141.4 12.8 %collective-permute-start.30 = (f32[64,64]{1,0:T(8,128)S(1)}, f32[64,64]{1,0:T(8,128)S(1)}, u32[]{:S(2)}, u32[]{:S(2)}) collective-permute-start(f32[64,64]{1,0:T(8,128)S(1)} %slice_add_fusion.1), channel_id=1, source_target_pairs={{0,1},{1,0},{2,3},{3,2},{4,5},{5,4},{6,7},{7,6},{8,9},{9,8},{10,11... | collective-permute-start | bytes 49160 | tf_op jit(solution)/shard_map/ppermute | solution.py:30
  154.2 0.9 collective-permute-done.30
  155.4 3.7 %collective-permute-done.31 = f32[64,64]{1,0:T(8,128)S(1)} collective-permute-done((f32[64,64]{1,0:T(8,128)S(1)}, f32[64,64]{1,0:T(8,128)S(1)}, u32[]{:S(2)}, u32[]{:S(2)}) %collective-permute-start.31) | collective-permute-done | bytes 16416 | tf_op jit(solution)/shard_map/ppermute | solution.py:30
  159.1 0.5 collective-permute-start.32
  159.6 3.4 %collective-permute-done.32 = f32[64,64]{1,0:T(8,128)S(1)} collective-permute-done((f32[64,64]{1,0:T(8,128)S(1)}, f32[64,64]{1,0:T(8,128)S(1)}, u32[]{:S(2)}, u32[]{:S(2)}) %collective-permute-start.32) | collective-permute-done | bytes 16416 | tf_op jit(solution)/shard_map/ppermute | solution.py:30
  163.1 1.5 collective-permute-start.33
  164.6 3.6 %collective-permute-done.33 = f32[64,64]{1,0:T(8,128)S(1)} collective-permute-done((f32[64,64]{1,0:T(8,128)S(1)}, f32[64,64]{1,0:T(8,128)S(1)}, u32[]{:S(2)}, u32[]{:S(2)}) %collective-permute-start.33) | collective-permute-done | bytes 16416 | tf_op jit(solution)/shard_map/ppermute | solution.py:30
  168.2 2.6 %factor.3 = (bf16[64,384]{1,0:T(8,128)(2,1)S(1)}, f32[1,64]{1,0:T(1,128)}) custom-call(f32[64,64]{1,0:T(8,128)S(1)} %add.94.refs_0_, f32[1,64]{1,0:T(1,128)S(1)} %get-tuple-element.118.refs_1_), custom_call_target="tpu_custom_call" | custom-call | tf_op jit(solution)/shard_map/factor/pallas_call | solution.py:244
  170.7 4.3 %finish.1 = f32[64,2,96,128]{3,2,1,0:T(8,128)} custom-call(bf16[64,384]{1,0:T(8,128)(2,1)S(1)} %get-tuple-element.119.inverse_ref, f32[96,2,64,128]{3,2,1,0:T(8,128)S(1)} %get-tuple-element.120.partial_ref), custom_call_target="tpu_custom_call" | custom-call | tf_op jit(solution)/shard_map/finish/pallas_call | solution.py:522
  (72 shorter events, 2.5 us)
Async XLA Ops:
  0.6 2.8 %copy-start = (f32[64,2,96,128]{3,2,1,0:T(8,128)S(1)}, f32[64,2,96,128]{3,2,1,0:T(8,128)}, u32[]{:S(2)}) copy-start(f32[64,2,96,128]{3,2,1,0:T(8,128)} %vectors_ref.24) | copy-start | bytes 18874372
  3.4 5.8 %copy-start.2 = (f32[2,96,128]{2,1,0:T(8,128)S(1)}, f32[2,96,128]{2,1,0:T(8,128)}, u32[]{:S(2)}) copy-start(f32[2,96,128]{2,1,0:T(8,128)} %param.7) | copy-start | bytes 294916
  3.4 5.8 %copy-start.3 = (f32[2,96,128]{2,1,0:T(8,128)S(1)}, f32[2,96,128]{2,1,0:T(8,128)}, u32[]{:S(2)}) copy-start(f32[2,96,128]{2,1,0:T(8,128)} %param.6) | copy-start | bytes 294916
  3.4 5.8 %copy-start.4 = (f32[2,96,128]{2,1,0:T(8,128)S(1)}, f32[2,96,128]{2,1,0:T(8,128)}, u32[]{:S(2)}) copy-start(f32[2,96,128]{2,1,0:T(8,128)} %param.5) | copy-start | bytes 294916
  3.4 10.4 %copy-start.1 = (f32[64,2,96,128]{3,2,1,0:T(8,128)S(1)}, f32[64,2,96,128]{3,2,1,0:T(8,128)}, u32[]{:S(2)}) copy-start(f32[64,2,96,128]{3,2,1,0:T(8,128)} %vectors_ref.24) | copy-start | bytes 18874372
  3.7 26.7 %collective-permute-start.3 = (f32[2,8,64,128]{3,2,1,0:T(8,128)S(1)}, f32[2,8,64,128]{3,2,1,0:T(8,128)S(1)}, u32[]{:S(2)}, u32[]{:S(2)}) collective-permute-start(f32[2,8,64,128]{3,2,1,0:T(8,128)S(1)} %turn.13.refs_2_.refs_5_), channel_id=1, source_target_pairs={{0,1},{1,2},{2,3},{3,4},{4,5},{5,6},{6,7},{7,8},{8,9},{9,10},{10,1... | collective-permute-start | bytes 1572872 | tf_op jit(solution)/shard_map/ppermute | solution.py:26
  4.2 26.7 %collective-permute-start.4 = (f32[2,8,64,128]{3,2,1,0:T(8,128)S(1)}, f32[2,8,64,128]{3,2,1,0:T(8,128)S(1)}, u32[]{:S(2)}, u32[]{:S(2)}) collective-permute-start(f32[2,8,64,128]{3,2,1,0:T(8,128)S(1)} %turn.13.refs_2_.refs_5_), channel_id=1, source_target_pairs={{0,15},{1,0},{2,1},{3,2},{4,3},{5,4},{6,5},{7,6},{8,7},{9,8},{10,9... | collective-permute-start | bytes 1572872 | tf_op jit(solution)/shard_map/ppermute | solution.py:26
  9.3 15.8 %collective-permute-start.1 = (f32[1,3,96,128]{3,2,0,1:T(8,128)S(1)}, f32[1,3,96,128]{3,2,0,1:T(8,128)S(1)}, u32[]{:S(2)}, u32[]{:S(2)}) collective-permute-start(f32[1,3,96,128]{3,2,0,1:T(8,128)S(1)} %get-tuple-element.128), channel_id=1, source_target_pairs={{0,1},{1,2},{2,3},{3,4},{4,5},{5,6},{6,7},{7,8},{8,9},{9,10},{10,1... | collective-permute-start | bytes 442376 | tf_op jit(solution)/shard_map/ppermute | solution.py:26
  9.4 20.2 %collective-permute-start.2 = (f32[1,3,96,128]{3,2,0,1:T(8,128)S(1)}, f32[1,3,96,128]{3,2,0,1:T(8,128)S(1)}, u32[]{:S(2)}, u32[]{:S(2)}) collective-permute-start(f32[1,3,96,128]{3,2,0,1:T(8,128)S(1)} %get-tuple-element.129), channel_id=1, source_target_pairs={{0,15},{1,0},{2,1},{3,2},{4,3},{5,4},{6,5},{7,6},{8,7},{9,8},{10,9... | collective-permute-start | bytes 442376 | tf_op jit(solution)/shard_map/ppermute | solution.py:26
  20.6 4.4 %collective-permute-start = (f32[64,64]{1,0:T(8,128)S(1)}, f32[64,64]{1,0:T(8,128)S(1)}, u32[]{:S(2)}, u32[]{:S(2)}) collective-permute-start(f32[64,64]{1,0:T(8,128)S(1)} %gram.1), channel_id=1, source_target_pairs={{0,2},{1,3},{2,0},{3,1},{4,6},{5,7},{6,4},{7,5},{8,10},{9,11},{10,... | collective-permute-start | bytes 49160 | tf_op jit(solution)/shard_map/ppermute | solution.py:30
  25.1 11.4 %collective-permute-start.6 = (f32[2,8,64,128]{3,2,1,0:T(8,128)S(1)}, f32[2,8,64,128]{3,2,1,0:T(8,128)S(1)}, u32[]{:S(2)}, u32[]{:S(2)}) collective-permute-start(f32[2,8,64,128]{3,2,1,0:T(8,128)S(1)} %turn.12.refs_2_.refs_5_), channel_id=1, source_target_pairs={{0,1},{1,2},{2,3},{3,4},{4,5},{5,6},{6,7},{7,8},{8,9},{9,10},{10,1... | collective-permute-start | bytes 1572872 | tf_op jit(solution)/shard_map/ppermute | solution.py:26
  25.1 12.9 %collective-permute-start.7 = (f32[2,8,64,128]{3,2,1,0:T(8,128)S(1)}, f32[2,8,64,128]{3,2,1,0:T(8,128)S(1)}, u32[]{:S(2)}, u32[]{:S(2)}) collective-permute-start(f32[2,8,64,128]{3,2,1,0:T(8,128)S(1)} %turn.12.refs_2_.refs_5_), channel_id=1, source_target_pairs={{0,15},{1,0},{2,1},{3,2},{4,3},{5,4},{6,5},{7,6},{8,7},{9,8},{10,9... | collective-permute-start | bytes 1572872 | tf_op jit(solution)/shard_map/ppermute | solution.py:26
  29.6 25.3 %collective-permute-start.10 = (f32[2,8,64,128]{3,2,1,0:T(8,128)S(1)}, f32[2,8,64,128]{3,2,1,0:T(8,128)S(1)}, u32[]{:S(2)}, u32[]{:S(2)}) collective-permute-start(f32[2,8,64,128]{3,2,1,0:T(8,128)S(1)} %turn.14.refs_2_.refs_5_), channel_id=1, source_target_pairs={{0,15},{1,0},{2,1},{3,2},{4,3},{5,4},{6,5},{7,6},{8,7},{9,8},{10,9... | collective-permute-start | bytes 1572872 | tf_op jit(solution)/shard_map/ppermute | solution.py:26
  30.4 25.4 %collective-permute-start.9 = (f32[2,8,64,128]{3,2,1,0:T(8,128)S(1)}, f32[2,8,64,128]{3,2,1,0:T(8,128)S(1)}, u32[]{:S(2)}, u32[]{:S(2)}) collective-permute-start(f32[2,8,64,128]{3,2,1,0:T(8,128)S(1)} %turn.14.refs_2_.refs_5_), channel_id=1, source_target_pairs={{0,1},{1,2},{2,3},{3,4},{4,5},{5,6},{6,7},{7,8},{8,9},{9,10},{10,1... | collective-permute-start | bytes 1572872 | tf_op jit(solution)/shard_map/ppermute | solution.py:26
  32.2 1.3 collective-permute-start.5
  33.5 31.3 %collective-permute-start.14 = (f32[2,8,64,128]{3,2,1,0:T(8,128)S(1)}, f32[2,8,64,128]{3,2,1,0:T(8,128)S(1)}, u32[]{:S(2)}, u32[]{:S(2)}) collective-permute-start(f32[2,8,64,128]{3,2,1,0:T(8,128)S(1)} %turn.16.refs_2_.refs_5_), channel_id=1, source_target_pairs={{0,1},{1,2},{2,3},{3,4},{4,5},{5,6},{6,7},{7,8},{8,9},{9,10},{10,1... | collective-permute-start | bytes 1572872 | tf_op jit(solution)/shard_map/ppermute | solution.py:26
  36.5 33.0 %collective-permute-start.15 = (f32[2,8,64,128]{3,2,1,0:T(8,128)S(1)}, f32[2,8,64,128]{3,2,1,0:T(8,128)S(1)}, u32[]{:S(2)}, u32[]{:S(2)}) collective-permute-start(f32[2,8,64,128]{3,2,1,0:T(8,128)S(1)} %turn.16.refs_2_.refs_5_), channel_id=1, source_target_pairs={{0,15},{1,0},{2,1},{3,2},{4,3},{5,4},{6,5},{7,6},{8,7},{9,8},{10,9... | collective-permute-start | bytes 1572872 | tf_op jit(solution)/shard_map/ppermute | solution.py:26
  39.6 8.3 %collective-permute-start.8 = (f32[64,64]{1,0:T(8,128)S(1)}, f32[64,64]{1,0:T(8,128)S(1)}, u32[]{:S(2)}, u32[]{:S(2)}) collective-permute-start(f32[64,64]{1,0:T(8,128)S(1)} %add.85), channel_id=1, source_target_pairs={{0,4},{1,5},{2,6},{3,7},{4,0},{5,1},{6,2},{7,3},{8,12},{9,13},{10,... | collective-permute-start | bytes 49160 | tf_op jit(solution)/shard_map/ppermute | solution.py:30
  47.9 23.3 %collective-permute-start.12 = (f32[2,8,64,128]{3,2,1,0:T(8,128)S(1)}, f32[2,8,64,128]{3,2,1,0:T(8,128)S(1)}, u32[]{:S(2)}, u32[]{:S(2)}) collective-permute-start(f32[2,8,64,128]{3,2,1,0:T(8,128)S(1)} %turn.15.refs_2_.refs_5_), channel_id=1, source_target_pairs={{0,1},{1,2},{2,3},{3,4},{4,5},{5,6},{6,7},{7,8},{8,9},{9,10},{10,1... | collective-permute-start | bytes 1572872 | tf_op jit(solution)/shard_map/ppermute | solution.py:26
  54.9 21.5 %collective-permute-start.13 = (f32[2,8,64,128]{3,2,1,0:T(8,128)S(1)}, f32[2,8,64,128]{3,2,1,0:T(8,128)S(1)}, u32[]{:S(2)}, u32[]{:S(2)}) collective-permute-start(f32[2,8,64,128]{3,2,1,0:T(8,128)S(1)} %turn.15.refs_2_.refs_5_), channel_id=1, source_target_pairs={{0,15},{1,0},{2,1},{3,2},{4,3},{5,4},{6,5},{7,6},{8,7},{9,8},{10,9... | collective-permute-start | bytes 1572872 | tf_op jit(solution)/shard_map/ppermute | solution.py:26
  57.4 7.4 %collective-permute-start.11 = (f32[64,64]{1,0:T(8,128)S(1)}, f32[64,64]{1,0:T(8,128)S(1)}, u32[]{:S(2)}, u32[]{:S(2)}) collective-permute-start(f32[64,64]{1,0:T(8,128)S(1)} %add.86), channel_id=1, source_target_pairs={{0,8},{1,9},{2,10},{3,11},{4,12},{5,13},{6,14},{7,15},{8,0},{9,1},... | collective-permute-start | bytes 49160 | tf_op jit(solution)/shard_map/ppermute | solution.py:30
  64.8 23.0 %collective-permute-start.16 = (f32[2,8,64,128]{3,2,1,0:T(8,128)S(1)}, f32[2,8,64,128]{3,2,1,0:T(8,128)S(1)}, u32[]{:S(2)}, u32[]{:S(2)}) collective-permute-start(f32[2,8,64,128]{3,2,1,0:T(8,128)S(1)} %turn.19.refs_2_.refs_5_), channel_id=1, source_target_pairs={{0,1},{1,2},{2,3},{3,4},{4,5},{5,6},{6,7},{7,8},{8,9},{9,10},{10,1... | collective-permute-start | bytes 1572872 | tf_op jit(solution)/shard_map/ppermute | solution.py:26
  64.8 23.0 %collective-permute-start.17 = (f32[2,8,64,128]{3,2,1,0:T(8,128)S(1)}, f32[2,8,64,128]{3,2,1,0:T(8,128)S(1)}, u32[]{:S(2)}, u32[]{:S(2)}) collective-permute-start(f32[2,8,64,128]{3,2,1,0:T(8,128)S(1)} %turn.19.refs_2_.refs_5_), channel_id=1, source_target_pairs={{0,15},{1,0},{2,1},{3,2},{4,3},{5,4},{6,5},{7,6},{8,7},{9,8},{10,9... | collective-permute-start | bytes 1572872 | tf_op jit(solution)/shard_map/ppermute | solution.py:26
  71.1 29.4 %collective-permute-start.22 = (f32[2,8,64,128]{3,2,1,0:T(8,128)S(1)}, f32[2,8,64,128]{3,2,1,0:T(8,128)S(1)}, u32[]{:S(2)}, u32[]{:S(2)}) collective-permute-start(f32[2,8,64,128]{3,2,1,0:T(8,128)S(1)} %turn.21.refs_2_.refs_5_), channel_id=1, source_target_pairs={{0,1},{1,2},{2,3},{3,4},{4,5},{5,6},{6,7},{7,8},{8,9},{9,10},{10,1... | collective-permute-start | bytes 1572872 | tf_op jit(solution)/shard_map/ppermute | solution.py:26
  71.2 29.4 %collective-permute-start.23 = (f32[2,8,64,128]{3,2,1,0:T(8,128)S(1)}, f32[2,8,64,128]{3,2,1,0:T(8,128)S(1)}, u32[]{:S(2)}, u32[]{:S(2)}) collective-permute-start(f32[2,8,64,128]{3,2,1,0:T(8,128)S(1)} %turn.21.refs_2_.refs_5_), channel_id=1, source_target_pairs={{0,15},{1,0},{2,1},{3,2},{4,3},{5,4},{6,5},{7,6},{8,7},{9,8},{10,9... | collective-permute-start | bytes 1572872 | tf_op jit(solution)/shard_map/ppermute | solution.py:26
  80.0 28.7 %collective-permute-start.20 = (f32[2,8,64,128]{3,2,1,0:T(8,128)S(1)}, f32[2,8,64,128]{3,2,1,0:T(8,128)S(1)}, u32[]{:S(2)}, u32[]{:S(2)}) collective-permute-start(f32[2,8,64,128]{3,2,1,0:T(8,128)S(1)} %turn.20.refs_2_.refs_5_), channel_id=1, source_target_pairs={{0,1},{1,2},{2,3},{3,4},{4,5},{5,6},{6,7},{7,8},{8,9},{9,10},{10,1... | collective-permute-start | bytes 1572872 | tf_op jit(solution)/shard_map/ppermute | solution.py:26
  87.8 21.6 %collective-permute-start.21 = (f32[2,8,64,128]{3,2,1,0:T(8,128)S(1)}, f32[2,8,64,128]{3,2,1,0:T(8,128)S(1)}, u32[]{:S(2)}, u32[]{:S(2)}) collective-permute-start(f32[2,8,64,128]{3,2,1,0:T(8,128)S(1)} %turn.20.refs_2_.refs_5_), channel_id=1, source_target_pairs={{0,15},{1,0},{2,1},{3,2},{4,3},{5,4},{6,5},{7,6},{8,7},{9,8},{10,9... | collective-permute-start | bytes 1572872 | tf_op jit(solution)/shard_map/ppermute | solution.py:26
  89.4 35.7 %collective-permute-start.18 = (f32[2,8,64,128]{3,2,1,0:T(8,128)S(1)}, f32[2,8,64,128]{3,2,1,0:T(8,128)S(1)}, u32[]{:S(2)}, u32[]{:S(2)}) collective-permute-start(f32[2,8,64,128]{3,2,1,0:T(8,128)S(1)} %turn.18.refs_2_.refs_5_), channel_id=1, source_target_pairs={{0,1},{1,2},{2,3},{3,4},{4,5},{5,6},{6,7},{7,8},{8,9},{9,10},{10,1... | collective-permute-start | bytes 1572872 | tf_op jit(solution)/shard_map/ppermute | solution.py:26
  100.6 25.1 %collective-permute-start.19 = (f32[2,8,64,128]{3,2,1,0:T(8,128)S(1)}, f32[2,8,64,128]{3,2,1,0:T(8,128)S(1)}, u32[]{:S(2)}, u32[]{:S(2)}) collective-permute-start(f32[2,8,64,128]{3,2,1,0:T(8,128)S(1)} %turn.18.refs_2_.refs_5_), channel_id=1, source_target_pairs={{0,15},{1,0},{2,1},{3,2},{4,3},{5,4},{6,5},{7,6},{8,7},{9,8},{10,9... | collective-permute-start | bytes 1572872 | tf_op jit(solution)/shard_map/ppermute | solution.py:26
  102.2 28.5 %collective-permute-start.28 = (f32[2,8,64,128]{3,2,1,0:T(8,128)S(1)}, f32[2,8,64,128]{3,2,1,0:T(8,128)S(1)}, u32[]{:S(2)}, u32[]{:S(2)}) collective-permute-start(f32[2,8,64,128]{3,2,1,0:T(8,128)S(1)} %turn.23.refs_2_.refs_5_), channel_id=1, source_target_pairs={{0,1},{1,2},{2,3},{3,4},{4,5},{5,6},{6,7},{7,8},{8,9},{9,10},{10,1... | collective-permute-start | bytes 1572872 | tf_op jit(solution)/shard_map/ppermute | solution.py:26
  108.8 23.7 %collective-permute-start.29 = (f32[2,8,64,128]{3,2,1,0:T(8,128)S(1)}, f32[2,8,64,128]{3,2,1,0:T(8,128)S(1)}, u32[]{:S(2)}, u32[]{:S(2)}) collective-permute-start(f32[2,8,64,128]{3,2,1,0:T(8,128)S(1)} %turn.23.refs_2_.refs_5_), channel_id=1, source_target_pairs={{0,15},{1,0},{2,1},{3,2},{4,3},{5,4},{6,5},{7,6},{8,7},{9,8},{10,9... | collective-permute-start | bytes 1572872 | tf_op jit(solution)/shard_map/ppermute | solution.py:26
  111.0 23.6 %collective-permute-start.26 = (f32[2,8,64,128]{3,2,1,0:T(8,128)S(1)}, f32[2,8,64,128]{3,2,1,0:T(8,128)S(1)}, u32[]{:S(2)}, u32[]{:S(2)}) collective-permute-start(f32[2,8,64,128]{3,2,1,0:T(8,128)S(1)} %turn.22.refs_2_.refs_5_), channel_id=1, source_target_pairs={{0,1},{1,2},{2,3},{3,4},{4,5},{5,6},{6,7},{7,8},{8,9},{9,10},{10,1... | collective-permute-start | bytes 1572872 | tf_op jit(solution)/shard_map/ppermute | solution.py:26
  125.1 9.5 %collective-permute-start.27 = (f32[2,8,64,128]{3,2,1,0:T(8,128)S(1)}, f32[2,8,64,128]{3,2,1,0:T(8,128)S(1)}, u32[]{:S(2)}, u32[]{:S(2)}) collective-permute-start(f32[2,8,64,128]{3,2,1,0:T(8,128)S(1)} %turn.22.refs_2_.refs_5_), channel_id=1, source_target_pairs={{0,15},{1,0},{2,1},{3,2},{4,3},{5,4},{6,5},{7,6},{8,7},{9,8},{10,9... | collective-permute-start | bytes 1572872 | tf_op jit(solution)/shard_map/ppermute | solution.py:26
  127.3 11.5 %collective-permute-start.24 = (f32[2,8,64,128]{3,2,1,0:T(8,128)S(1)}, f32[2,8,64,128]{3,2,1,0:T(8,128)S(1)}, u32[]{:S(2)}, u32[]{:S(2)}) collective-permute-start(f32[2,8,64,128]{3,2,1,0:T(8,128)S(1)} %turn.17.refs_2_), channel_id=1, source_target_pairs={{0,1},{1,2},{2,3},{3,4},{4,5},{5,6},{6,7},{7,8},{8,9},{9,10},{10,1... | collective-permute-start | bytes 1572872 | tf_op jit(solution)/shard_map/ppermute | solution.py:26
  130.7 8.1 %collective-permute-start.25 = (f32[2,8,64,128]{3,2,1,0:T(8,128)S(1)}, f32[2,8,64,128]{3,2,1,0:T(8,128)S(1)}, u32[]{:S(2)}, u32[]{:S(2)}) collective-permute-start(f32[2,8,64,128]{3,2,1,0:T(8,128)S(1)} %turn.17.refs_2_), channel_id=1, source_target_pairs={{0,15},{1,0},{2,1},{3,2},{4,3},{5,4},{6,5},{7,6},{8,7},{9,8},{10,9... | collective-permute-start | bytes 1572872 | tf_op jit(solution)/shard_map/ppermute | solution.py:26
  141.4 13.7 %collective-permute-start.30 = (f32[64,64]{1,0:T(8,128)S(1)}, f32[64,64]{1,0:T(8,128)S(1)}, u32[]{:S(2)}, u32[]{:S(2)}) collective-permute-start(f32[64,64]{1,0:T(8,128)S(1)} %slice_add_fusion.1), channel_id=1, source_target_pairs={{0,1},{1,0},{2,3},{3,2},{4,5},{5,4},{6,7},{7,6},{8,9},{9,8},{10,11... | collective-permute-start | bytes 49160 | tf_op jit(solution)/shard_map/ppermute | solution.py:30
  155.2 4.0 %collective-permute-start.31 = (f32[64,64]{1,0:T(8,128)S(1)}, f32[64,64]{1,0:T(8,128)S(1)}, u32[]{:S(2)}, u32[]{:S(2)}) collective-permute-start(f32[64,64]{1,0:T(8,128)S(1)} %fusion.12), channel_id=1, source_target_pairs={{0,2},{1,3},{2,0},{3,1},{4,6},{5,7},{6,4},{7,5},{8,10},{9,11},{10,... | collective-permute-start | bytes 49160 | tf_op jit(solution)/shard_map/ppermute | solution.py:30
  159.1 3.9 %collective-permute-start.32 = (f32[64,64]{1,0:T(8,128)S(1)}, f32[64,64]{1,0:T(8,128)S(1)}, u32[]{:S(2)}, u32[]{:S(2)}) collective-permute-start(f32[64,64]{1,0:T(8,128)S(1)} %add.92), channel_id=1, source_target_pairs={{0,4},{1,5},{2,6},{3,7},{4,0},{5,1},{6,2},{7,3},{8,12},{9,13},{10,... | collective-permute-start | bytes 49160 | tf_op jit(solution)/shard_map/ppermute | solution.py:30
  163.1 5.1 %collective-permute-start.33 = (f32[64,64]{1,0:T(8,128)S(1)}, f32[64,64]{1,0:T(8,128)S(1)}, u32[]{:S(2)}, u32[]{:S(2)}) collective-permute-start(f32[64,64]{1,0:T(8,128)S(1)} %add.93), channel_id=1, source_target_pairs={{0,8},{1,9},{2,10},{3,11},{4,12},{5,13},{6,14},{7,15},{8,0},{9,1},... | collective-permute-start | bytes 49160 | tf_op jit(solution)/shard_map/ppermute | solution.py:30

commit v2 on v1

--- a/solution.py
+++ b/solution.py
@@ -13,7 +13,7 @@
 BF16 = jnp.bfloat16
 ROWS = 8
 UNROLL = 8
-PIVOTS = 4
+PIVOTS = 8
 FUSED = 5
 HOP_EVERY = 1
 STEP = 0.3

time: 175 us -> 175 us (level)
  no operation moved by 1% of the time
where the time goes in v2:
time: 175 us
  starting transfers between devices  90.2 us (52%)
  Pallas kernels  43.8 us (25%)
  waiting for transfers between devices  35.3 us (20%)
  local copies, waits for them, and re-layouts  3.34 us (2%)
    ppermute x26, starting transfers between devices, shift(): lax.ppermute(block, axis, [(i, (i + step) % count) for i in range(count)])  74.1 us
    ppermute x8, waiting for transfers between devices, exchange(): lax.ppermute(value, axis, [(i, i ^ hop) for i in range(lax.axis_size(axis...  30.5 us
    pallas_call x12, Pallas kernels, advance(): pl.pallas_call(functools.partial(advance_kernel, first, last, base - 2),...  19 us
    ppermute x8, starting transfers between devices, exchange(): lax.ppermute(value, axis, [(i, i ^ hop) for i in range(lax.axis_size(axis...  16.1 us
    pallas_call x7, Pallas kernels, mix(): pl.pallas_call(functools.partial(mix_kernel, start, stop), in_specs=[memo...  7.21 us
    pallas_call x1, Pallas kernels, gram_of(): pl.pallas_call(gram_kernel, in_specs=[pl.BlockSpec(memory_space=pltpu.HBM...  6.57 us
    ppermute x26, waiting for transfers between devices, shift(): lax.ppermute(block, axis, [(i, (i + step) % count) for i in range(count)])  4.8 us
    pallas_call x1, Pallas kernels, finish(): pl.pallas_call(finish_kernel, in_specs=[memory, memory], out_specs=pl.Blo...  4.33 us
  transfers between devices with their start and end apart: 34, of which 10 were waited for; matrix products, arithmetic and copies ran while one was open for 1% of the time, Pallas kernels for 20%

profile of v2, /device:TPU:0, one launch (start us, length us, event | category | flops | bytes accessed | tf_op | source)
XLA Modules:
  0.0 174.8 jit_solution(16015330326123598020)
XLA Ops:
  0.6 2.8 %copy-done = f32[64,2,96,128]{3,2,1,0:T(8,128)S(1)} copy-done((f32[64,2,96,128]{3,2,1,0:T(8,128)S(1)}, f32[64,2,96,128]{3,2,1,0:T(8,128)}, u32[]{:S(2)}) %copy-start) | copy-done | bytes 6291480
  3.4 0.2 turn.13.refs_2_.refs_5_
  3.7 0.5 collective-permute-start.3
  4.2 5.1 %collective-permute-start.4 = (f32[2,8,64,128]{3,2,1,0:T(8,128)S(1)}, f32[2,8,64,128]{3,2,1,0:T(8,128)S(1)}, u32[]{:S(2)}, u32[]{:S(2)}) collective-permute-start(f32[2,8,64,128]{3,2,1,0:T(8,128)S(1)} %turn.13.refs_2_.refs_5_), channel_id=1, source_target_pairs={{0,15},{1,0},{2,1},{3,2},{4,3},{5,4},{6,5},{7,6},{8,7},{9,8},{10,9... | collective-permute-start | bytes 1572872 | tf_op jit(solution)/shard_map/ppermute | solution.py:26
  9.4 4.4 %collective-permute-start.2 = (f32[1,3,96,128]{3,2,0,1:T(8,128)S(1)}, f32[1,3,96,128]{3,2,0,1:T(8,128)S(1)}, u32[]{:S(2)}, u32[]{:S(2)}) collective-permute-start(f32[1,3,96,128]{3,2,0,1:T(8,128)S(1)} %get-tuple-element.129), channel_id=1, source_target_pairs={{0,15},{1,0},{2,1},{3,2},{4,3},{5,4},{6,5},{7,6},{8,7},{9,8},{10,9... | collective-permute-start | bytes 442376 | tf_op jit(solution)/shard_map/ppermute | solution.py:26
  13.8 0.2 turn.12.refs_2_.refs_5_
  14.1 6.6 %gram.1 = f32[64,64]{1,0:T(8,128)S(1)} custom-call(f32[64,2,96,128]{3,2,1,0:T(8,128)S(1)} %copy-done.1), custom_call_target="tpu_custom_call" | custom-call | flops 1207959552 | bytes 6291456 | tf_op jit(solution)/shard_map/gram/pallas_call | solution.py:173
  20.7 0.3 multiply_select_fusion
  21.2 0.2 turn.14.refs_2_.refs_5_
  21.4 3.6 %collective-permute-done = f32[64,64]{1,0:T(8,128)S(1)} collective-permute-done((f32[64,64]{1,0:T(8,128)S(1)}, f32[64,64]{1,0:T(8,128)S(1)}, u32[]{:S(2)}, u32[]{:S(2)}) %collective-permute-start) | collective-permute-done | bytes 16416 | tf_op jit(solution)/shard_map/ppermute | solution.py:30
  25.1 4.5 %collective-permute-start.7 = (f32[2,8,64,128]{3,2,1,0:T(8,128)S(1)}, f32[2,8,64,128]{3,2,1,0:T(8,128)S(1)}, u32[]{:S(2)}, u32[]{:S(2)}) collective-permute-start(f32[2,8,64,128]{3,2,1,0:T(8,128)S(1)} %turn.12.refs_2_.refs_5_), channel_id=1, source_target_pairs={{0,15},{1,0},{2,1},{3,2},{4,3},{5,4},{6,5},{7,6},{8,7},{9,8},{10,9... | collective-permute-start | bytes 1572872 | tf_op jit(solution)/shard_map/ppermute | solution.py:26
  29.9 0.5 copy.24
  30.4 0.5 collective-permute-start.9
  30.9 1.3 advance.12
  32.6 0.9 collective-permute-done.5
  33.7 2.8 %collective-permute-done.6.refs_3_.refs_6_ = f32[2,8,64,128]{3,2,1,0:T(8,128)S(1)} collective-permute-done((f32[2,8,64,128]{3,2,1,0:T(8,128)S(1)}, f32[2,8,64,128]{3,2,1,0:T(8,128)S(1)}, u32[]{:S(2)}, u32[]{:S(2)}) %collective-permute-start.6) | collective-permute-done | bytes 524320 | tf_op jit(solution)/shard_map/ppermute | solution.py:26
  36.5 1.5 collective-permute-start.15
  38.0 1.6 advance.13
  39.7 0.2 turn.15.refs_2_.refs_5_
  39.9 8.0 %collective-permute-done.8 = f32[64,64]{1,0:T(8,128)S(1)} collective-permute-done((f32[64,64]{1,0:T(8,128)S(1)}, f32[64,64]{1,0:T(8,128)S(1)}, u32[]{:S(2)}, u32[]{:S(2)}) %collective-permute-start.8) | collective-permute-done | bytes 16416 | tf_op jit(solution)/shard_map/ppermute | solution.py:30
  47.9 6.9 %collective-permute-start.12 = (f32[2,8,64,128]{3,2,1,0:T(8,128)S(1)}, f32[2,8,64,128]{3,2,1,0:T(8,128)S(1)}, u32[]{:S(2)}, u32[]{:S(2)}) collective-permute-start(f32[2,8,64,128]{3,2,1,0:T(8,128)S(1)} %turn.15.refs_2_.refs_5_), channel_id=1, source_target_pairs={{0,1},{1,2},{2,3},{3,4},{4,5},{5,6},{6,7},{7,8},{8,9},{9,10},{10,1... | collective-permute-start | bytes 1572872 | tf_op jit(solution)/shard_map/ppermute | solution.py:26
  54.9 1.0 collective-permute-start.13
  55.8 1.6 advance.14
  57.4 0.8 collective-permute-start.11
  58.2 0.2 turn.19.refs_2_.refs_5_
  58.5 6.3 %collective-permute-done.11 = f32[64,64]{1,0:T(8,128)S(1)} collective-permute-done((f32[64,64]{1,0:T(8,128)S(1)}, f32[64,64]{1,0:T(8,128)S(1)}, u32[]{:S(2)}, u32[]{:S(2)}) %collective-permute-start.11) | collective-permute-done | bytes 16416 | tf_op jit(solution)/shard_map/ppermute | solution.py:30
  64.8 4.4 %collective-permute-start.17 = (f32[2,8,64,128]{3,2,1,0:T(8,128)S(1)}, f32[2,8,64,128]{3,2,1,0:T(8,128)S(1)}, u32[]{:S(2)}, u32[]{:S(2)}) collective-permute-start(f32[2,8,64,128]{3,2,1,0:T(8,128)S(1)} %turn.19.refs_2_.refs_5_), channel_id=1, source_target_pairs={{0,15},{1,0},{2,1},{3,2},{4,3},{5,4},{6,5},{7,6},{8,7},{9,8},{10,9... | collective-permute-start | bytes 1572872 | tf_op jit(solution)/shard_map/ppermute | solution.py:26
  69.5 1.6 advance.15
  71.2 4.4 %collective-permute-start.23 = (f32[2,8,64,128]{3,2,1,0:T(8,128)S(1)}, f32[2,8,64,128]{3,2,1,0:T(8,128)S(1)}, u32[]{:S(2)}, u32[]{:S(2)}) collective-permute-start(f32[2,8,64,128]{3,2,1,0:T(8,128)S(1)} %turn.21.refs_2_.refs_5_), channel_id=1, source_target_pairs={{0,15},{1,0},{2,1},{3,2},{4,3},{5,4},{6,5},{7,6},{8,7},{9,8},{10,9... | collective-permute-start | bytes 1572872 | tf_op jit(solution)/shard_map/ppermute | solution.py:26
  75.9 0.2 turn.18.refs_2_.refs_5_
  76.1 0.2 turn.23.refs_2_.refs_5_
  76.4 1.6 advance.16
  78.0 1.7 factor.2
  79.6 7.8 %collective-permute-start.20 = (f32[2,8,64,128]{3,2,1,0:T(8,128)S(1)}, f32[2,8,64,128]{3,2,1,0:T(8,128)S(1)}, u32[]{:S(2)}, u32[]{:S(2)}) collective-permute-start(f32[2,8,64,128]{3,2,1,0:T(8,128)S(1)} %turn.20.refs_2_.refs_5_), channel_id=1, source_target_pairs={{0,1},{1,2},{2,3},{3,4},{4,5},{5,6},{6,7},{7,8},{8,9},{9,10},{10,1... | collective-permute-start | bytes 1572872 | tf_op jit(solution)/shard_map/ppermute | solution.py:26
  87.4 1.6 advance.17
  89.0 8.0 %collective-permute-start.18 = (f32[2,8,64,128]{3,2,1,0:T(8,128)S(1)}, f32[2,8,64,128]{3,2,1,0:T(8,128)S(1)}, u32[]{:S(2)}, u32[]{:S(2)}) collective-permute-start(f32[2,8,64,128]{3,2,1,0:T(8,128)S(1)} %turn.18.refs_2_.refs_5_), channel_id=1, source_target_pairs={{0,1},{1,2},{2,3},{3,4},{4,5},{5,6},{6,7},{7,8},{8,9},{9,10},{10,1... | collective-permute-start | bytes 1572872 | tf_op jit(solution)/shard_map/ppermute | solution.py:26
  97.0 3.5 %mix.7 = (f32[96,2,64,128]{3,2,1,0:T(8,128)S(1)}, f32[128,128]{1,0:T(8,128)S(1)}) custom-call(bf16[64,384]{1,0:T(8,128)(2,1)S(1)} %get-tuple-element.84.mixer_ref, f32[96,2,64,128]{3,2,1,0:T(8,128)S(1)} %get-tuple-element.91._), custom_call_target="tpu_custom_call", output_to_operand_aliasing={{0}: (1, {})} | custom-call | flops 964689920 | bytes 6029312 | tf_op jit(solution)/shard_map/mix/pallas_call | solution.py:305
  100.6 1.6 advance.18
  102.2 6.0 %collective-permute-start.28 = (f32[2,8,64,128]{3,2,1,0:T(8,128)S(1)}, f32[2,8,64,128]{3,2,1,0:T(8,128)S(1)}, u32[]{:S(2)}, u32[]{:S(2)}) collective-permute-start(f32[2,8,64,128]{3,2,1,0:T(8,128)S(1)} %turn.23.refs_2_.refs_5_), channel_id=1, source_target_pairs={{0,1},{1,2},{2,3},{3,4},{4,5},{5,6},{6,7},{7,8},{8,9},{9,10},{10,1... | collective-permute-start | bytes 1572872 | tf_op jit(solution)/shard_map/ppermute | solution.py:26
  108.5 0.2 turn.17.refs_2_
  108.8 0.6 mix.8
  109.4 1.6 advance.19
  111.0 14.1 %collective-permute-start.26 = (f32[2,8,64,128]{3,2,1,0:T(8,128)S(1)}, f32[2,8,64,128]{3,2,1,0:T(8,128)S(1)}, u32[]{:S(2)}, u32[]{:S(2)}) collective-permute-start(f32[2,8,64,128]{3,2,1,0:T(8,128)S(1)} %turn.22.refs_2_.refs_5_), channel_id=1, source_target_pairs={{0,1},{1,2},{2,3},{3,4},{4,5},{5,6},{6,7},{7,8},{8,9},{9,10},{10,1... | collective-permute-start | bytes 1572872 | tf_op jit(solution)/shard_map/ppermute | solution.py:26
  125.1 0.6 mix.9
  125.7 1.6 advance.20
  127.3 3.4 %collective-permute-start.24 = (f32[2,8,64,128]{3,2,1,0:T(8,128)S(1)}, f32[2,8,64,128]{3,2,1,0:T(8,128)S(1)}, u32[]{:S(2)}, u32[]{:S(2)}) collective-permute-start(f32[2,8,64,128]{3,2,1,0:T(8,128)S(1)} %turn.17.refs_2_), channel_id=1, source_target_pairs={{0,1},{1,2},{2,3},{3,4},{4,5},{5,6},{6,7},{7,8},{8,9},{9,10},{10,1... | collective-permute-start | bytes 1572872 | tf_op jit(solution)/shard_map/ppermute | solution.py:26
  130.7 1.1 collective-permute-start.25
  131.8 0.6 mix.10
  132.4 1.6 advance.21
  134.0 0.6 mix.11
  134.6 1.6 advance.22
  136.2 0.6 mix.12
  136.8 1.9 %collective-permute-done.24.refs_3_ = f32[2,8,64,128]{3,2,1,0:T(8,128)S(1)} collective-permute-done((f32[2,8,64,128]{3,2,1,0:T(8,128)S(1)}, f32[2,8,64,128]{3,2,1,0:T(8,128)S(1)}, u32[]{:S(2)}, u32[]{:S(2)}) %collective-permute-start.24) | collective-permute-done | bytes 524320 | tf_op jit(solution)/shard_map/ppermute | solution.py:26
  138.8 1.8 %advance.23._ = f32[96,2,64,128]{3,2,1,0:T(8,128)S(1)} custom-call(bf16[768,256]{1,0:T(8,128)(2,1)S(1)} %fusion.8.refs_0_, f32[96,16,128]{2,1,0:T(8,128)S(1)} %bitcast.26, f32[2,8,64,128]{3,2,1,0:T(8,128)S(1)} %turn.17.refs_2_, f32[2,8,64,128]{3,2,1,0:T(8,128)S(1)} %collective-permute-done.24.refs_3_, ...), custom_call_target="tpu_custom_call", output_to_operand_aliasing={{}: (9, {})} | custom-call | flops 786432000 | bytes 2097152 | tf_op jit(solution)/shard_map/advance/pallas_call | solution.py:450
  140.6 0.7 mix.13
  141.4 12.8 %collective-permute-start.30 = (f32[64,64]{1,0:T(8,128)S(1)}, f32[64,64]{1,0:T(8,128)S(1)}, u32[]{:S(2)}, u32[]{:S(2)}) collective-permute-start(f32[64,64]{1,0:T(8,128)S(1)} %slice_add_fusion.1), channel_id=1, source_target_pairs={{0,1},{1,0},{2,3},{3,2},{4,5},{5,4},{6,7},{7,6},{8,9},{9,8},{10,11... | collective-permute-start | bytes 49160 | tf_op jit(solution)/shard_map/ppermute | solution.py:30
  154.2 0.9 collective-permute-done.30
  155.4 3.7 %collective-permute-done.31 = f32[64,64]{1,0:T(8,128)S(1)} collective-permute-done((f32[64,64]{1,0:T(8,128)S(1)}, f32[64,64]{1,0:T(8,128)S(1)}, u32[]{:S(2)}, u32[]{:S(2)}) %collective-permute-start.31) | collective-permute-done | bytes 16416 | tf_op jit(solution)/shard_map/ppermute | solution.py:30
  159.1 0.5 collective-permute-start.32
  159.6 3.4 %collective-permute-done.32 = f32[64,64]{1,0:T(8,128)S(1)} collective-permute-done((f32[64,64]{1,0:T(8,128)S(1)}, f32[64,64]{1,0:T(8,128)S(1)}, u32[]{:S(2)}, u32[]{:S(2)}) %collective-permute-start.32) | collective-permute-done | bytes 16416 | tf_op jit(solution)/shard_map/ppermute | solution.py:30
  163.1 1.5 collective-permute-start.33
  164.6 3.6 %collective-permute-done.33 = f32[64,64]{1,0:T(8,128)S(1)} collective-permute-done((f32[64,64]{1,0:T(8,128)S(1)}, f32[64,64]{1,0:T(8,128)S(1)}, u32[]{:S(2)}, u32[]{:S(2)}) %collective-permute-start.33) | collective-permute-done | bytes 16416 | tf_op jit(solution)/shard_map/ppermute | solution.py:30
  168.2 2.2 %factor.3 = (bf16[64,384]{1,0:T(8,128)(2,1)S(1)}, f32[1,64]{1,0:T(1,128)}) custom-call(f32[64,64]{1,0:T(8,128)S(1)} %add.94.refs_0_, f32[1,64]{1,0:T(1,128)S(1)} %get-tuple-element.118.refs_1_), custom_call_target="tpu_custom_call" | custom-call | tf_op jit(solution)/shard_map/factor/pallas_call | solution.py:244
  170.3 4.3 %finish.1 = f32[64,2,96,128]{3,2,1,0:T(8,128)} custom-call(bf16[64,384]{1,0:T(8,128)(2,1)S(1)} %get-tuple-element.119.inverse_ref, f32[96,2,64,128]{3,2,1,0:T(8,128)S(1)} %get-tuple-element.120.partial_ref), custom_call_target="tpu_custom_call" | custom-call | tf_op jit(solution)/shard_map/finish/pallas_call | solution.py:522
  (72 shorter events, 2.5 us)
Async XLA Ops:
  0.6 2.8 %copy-start = (f32[64,2,96,128]{3,2,1,0:T(8,128)S(1)}, f32[64,2,96,128]{3,2,1,0:T(8,128)}, u32[]{:S(2)}) copy-start(f32[64,2,96,128]{3,2,1,0:T(8,128)} %vectors_ref.24) | copy-start | bytes 18874372
  3.4 5.8 %copy-start.2 = (f32[2,96,128]{2,1,0:T(8,128)S(1)}, f32[2,96,128]{2,1,0:T(8,128)}, u32[]{:S(2)}) copy-start(f32[2,96,128]{2,1,0:T(8,128)} %param.7) | copy-start | bytes 294916
  3.4 5.8 %copy-start.3 = (f32[2,96,128]{2,1,0:T(8,128)S(1)}, f32[2,96,128]{2,1,0:T(8,128)}, u32[]{:S(2)}) copy-start(f32[2,96,128]{2,1,0:T(8,128)} %param.6) | copy-start | bytes 294916
  3.4 5.8 %copy-start.4 = (f32[2,96,128]{2,1,0:T(8,128)S(1)}, f32[2,96,128]{2,1,0:T(8,128)}, u32[]{:S(2)}) copy-start(f32[2,96,128]{2,1,0:T(8,128)} %param.5) | copy-start | bytes 294916
  3.4 10.4 %copy-start.1 = (f32[64,2,96,128]{3,2,1,0:T(8,128)S(1)}, f32[64,2,96,128]{3,2,1,0:T(8,128)}, u32[]{:S(2)}) copy-start(f32[64,2,96,128]{3,2,1,0:T(8,128)} %vectors_ref.24) | copy-start | bytes 18874372
  3.7 26.7 %collective-permute-start.3 = (f32[2,8,64,128]{3,2,1,0:T(8,128)S(1)}, f32[2,8,64,128]{3,2,1,0:T(8,128)S(1)}, u32[]{:S(2)}, u32[]{:S(2)}) collective-permute-start(f32[2,8,64,128]{3,2,1,0:T(8,128)S(1)} %turn.13.refs_2_.refs_5_), channel_id=1, source_target_pairs={{0,1},{1,2},{2,3},{3,4},{4,5},{5,6},{6,7},{7,8},{8,9},{9,10},{10,1... | collective-permute-start | bytes 1572872 | tf_op jit(solution)/shard_map/ppermute | solution.py:26
  4.2 26.7 %collective-permute-start.4 = (f32[2,8,64,128]{3,2,1,0:T(8,128)S(1)}, f32[2,8,64,128]{3,2,1,0:T(8,128)S(1)}, u32[]{:S(2)}, u32[]{:S(2)}) collective-permute-start(f32[2,8,64,128]{3,2,1,0:T(8,128)S(1)} %turn.13.refs_2_.refs_5_), channel_id=1, source_target_pairs={{0,15},{1,0},{2,1},{3,2},{4,3},{5,4},{6,5},{7,6},{8,7},{9,8},{10,9... | collective-permute-start | bytes 1572872 | tf_op jit(solution)/shard_map/ppermute | solution.py:26
  9.3 15.8 %collective-permute-start.1 = (f32[1,3,96,128]{3,2,0,1:T(8,128)S(1)}, f32[1,3,96,128]{3,2,0,1:T(8,128)S(1)}, u32[]{:S(2)}, u32[]{:S(2)}) collective-permute-start(f32[1,3,96,128]{3,2,0,1:T(8,128)S(1)} %get-tuple-element.128), channel_id=1, source_target_pairs={{0,1},{1,2},{2,3},{3,4},{4,5},{5,6},{6,7},{7,8},{8,9},{9,10},{10,1... | collective-permute-start | bytes 442376 | tf_op jit(solution)/shard_map/ppermute | solution.py:26
  9.4 20.2 %collective-permute-start.2 = (f32[1,3,96,128]{3,2,0,1:T(8,128)S(1)}, f32[1,3,96,128]{3,2,0,1:T(8,128)S(1)}, u32[]{:S(2)}, u32[]{:S(2)}) collective-permute-start(f32[1,3,96,128]{3,2,0,1:T(8,128)S(1)} %get-tuple-element.129), channel_id=1, source_target_pairs={{0,15},{1,0},{2,1},{3,2},{4,3},{5,4},{6,5},{7,6},{8,7},{9,8},{10,9... | collective-permute-start | bytes 442376 | tf_op jit(solution)/shard_map/ppermute | solution.py:26
  20.6 4.4 %collective-permute-start = (f32[64,64]{1,0:T(8,128)S(1)}, f32[64,64]{1,0:T(8,128)S(1)}, u32[]{:S(2)}, u32[]{:S(2)}) collective-permute-start(f32[64,64]{1,0:T(8,128)S(1)} %gram.1), channel_id=1, source_target_pairs={{0,2},{1,3},{2,0},{3,1},{4,6},{5,7},{6,4},{7,5},{8,10},{9,11},{10,... | collective-permute-start | bytes 49160 | tf_op jit(solution)/shard_map/ppermute | solution.py:30
  25.1 11.4 %collective-permute-start.6 = (f32[2,8,64,128]{3,2,1,0:T(8,128)S(1)}, f32[2,8,64,128]{3,2,1,0:T(8,128)S(1)}, u32[]{:S(2)}, u32[]{:S(2)}) collective-permute-start(f32[2,8,64,128]{3,2,1,0:T(8,128)S(1)} %turn.12.refs_2_.refs_5_), channel_id=1, source_target_pairs={{0,1},{1,2},{2,3},{3,4},{4,5},{5,6},{6,7},{7,8},{8,9},{9,10},{10,1... | collective-permute-start | bytes 1572872 | tf_op jit(solution)/shard_map/ppermute | solution.py:26
  25.1 12.9 %collective-permute-start.7 = (f32[2,8,64,128]{3,2,1,0:T(8,128)S(1)}, f32[2,8,64,128]{3,2,1,0:T(8,128)S(1)}, u32[]{:S(2)}, u32[]{:S(2)}) collective-permute-start(f32[2,8,64,128]{3,2,1,0:T(8,128)S(1)} %turn.12.refs_2_.refs_5_), channel_id=1, source_target_pairs={{0,15},{1,0},{2,1},{3,2},{4,3},{5,4},{6,5},{7,6},{8,7},{9,8},{10,9... | collective-permute-start | bytes 1572872 | tf_op jit(solution)/shard_map/ppermute | solution.py:26
  29.6 25.3 %collective-permute-start.10 = (f32[2,8,64,128]{3,2,1,0:T(8,128)S(1)}, f32[2,8,64,128]{3,2,1,0:T(8,128)S(1)}, u32[]{:S(2)}, u32[]{:S(2)}) collective-permute-start(f32[2,8,64,128]{3,2,1,0:T(8,128)S(1)} %turn.14.refs_2_.refs_5_), channel_id=1, source_target_pairs={{0,15},{1,0},{2,1},{3,2},{4,3},{5,4},{6,5},{7,6},{8,7},{9,8},{10,9... | collective-permute-start | bytes 1572872 | tf_op jit(solution)/shard_map/ppermute | solution.py:26
  30.4 25.4 %collective-permute-start.9 = (f32[2,8,64,128]{3,2,1,0:T(8,128)S(1)}, f32[2,8,64,128]{3,2,1,0:T(8,128)S(1)}, u32[]{:S(2)}, u32[]{:S(2)}) collective-permute-start(f32[2,8,64,128]{3,2,1,0:T(8,128)S(1)} %turn.14.refs_2_.refs_5_), channel_id=1, source_target_pairs={{0,1},{1,2},{2,3},{3,4},{4,5},{5,6},{6,7},{7,8},{8,9},{9,10},{10,1... | collective-permute-start | bytes 1572872 | tf_op jit(solution)/shard_map/ppermute | solution.py:26
  32.2 1.3 collective-permute-start.5
  33.5 31.3 %collective-permute-start.14 = (f32[2,8,64,128]{3,2,1,0:T(8,128)S(1)}, f32[2,8,64,128]{3,2,1,0:T(8,128)S(1)}, u32[]{:S(2)}, u32[]{:S(2)}) collective-permute-start(f32[2,8,64,128]{3,2,1,0:T(8,128)S(1)} %turn.16.refs_2_.refs_5_), channel_id=1, source_target_pairs={{0,1},{1,2},{2,3},{3,4},{4,5},{5,6},{6,7},{7,8},{8,9},{9,10},{10,1... | collective-permute-start | bytes 1572872 | tf_op jit(solution)/shard_map/ppermute | solution.py:26
  36.5 33.0 %collective-permute-start.15 = (f32[2,8,64,128]{3,2,1,0:T(8,128)S(1)}, f32[2,8,64,128]{3,2,1,0:T(8,128)S(1)}, u32[]{:S(2)}, u32[]{:S(2)}) collective-permute-start(f32[2,8,64,128]{3,2,1,0:T(8,128)S(1)} %turn.16.refs_2_.refs_5_), channel_id=1, source_target_pairs={{0,15},{1,0},{2,1},{3,2},{4,3},{5,4},{6,5},{7,6},{8,7},{9,8},{10,9... | collective-permute-start | bytes 1572872 | tf_op jit(solution)/shard_map/ppermute | solution.py:26
  39.6 8.3 %collective-permute-start.8 = (f32[64,64]{1,0:T(8,128)S(1)}, f32[64,64]{1,0:T(8,128)S(1)}, u32[]{:S(2)}, u32[]{:S(2)}) collective-permute-start(f32[64,64]{1,0:T(8,128)S(1)} %add.85), channel_id=1, source_target_pairs={{0,4},{1,5},{2,6},{3,7},{4,0},{5,1},{6,2},{7,3},{8,12},{9,13},{10,... | collective-permute-start | bytes 49160 | tf_op jit(solution)/shard_map/ppermute | solution.py:30
  47.9 23.3 %collective-permute-start.12 = (f32[2,8,64,128]{3,2,1,0:T(8,128)S(1)}, f32[2,8,64,128]{3,2,1,0:T(8,128)S(1)}, u32[]{:S(2)}, u32[]{:S(2)}) collective-permute-start(f32[2,8,64,128]{3,2,1,0:T(8,128)S(1)} %turn.15.refs_2_.refs_5_), channel_id=1, source_target_pairs={{0,1},{1,2},{2,3},{3,4},{4,5},{5,6},{6,7},{7,8},{8,9},{9,10},{10,1... | collective-permute-start | bytes 1572872 | tf_op jit(solution)/shard_map/ppermute | solution.py:26
  54.9 21.5 %collective-permute-start.13 = (f32[2,8,64,128]{3,2,1,0:T(8,128)S(1)}, f32[2,8,64,128]{3,2,1,0:T(8,128)S(1)}, u32[]{:S(2)}, u32[]{:S(2)}) collective-permute-start(f32[2,8,64,128]{3,2,1,0:T(8,128)S(1)} %turn.15.refs_2_.refs_5_), channel_id=1, source_target_pairs={{0,15},{1,0},{2,1},{3,2},{4,3},{5,4},{6,5},{7,6},{8,7},{9,8},{10,9... | collective-permute-start | bytes 1572872 | tf_op jit(solution)/shard_map/ppermute | solution.py:26
  57.4 7.4 %collective-permute-start.11 = (f32[64,64]{1,0:T(8,128)S(1)}, f32[64,64]{1,0:T(8,128)S(1)}, u32[]{:S(2)}, u32[]{:S(2)}) collective-permute-start(f32[64,64]{1,0:T(8,128)S(1)} %add.86), channel_id=1, source_target_pairs={{0,8},{1,9},{2,10},{3,11},{4,12},{5,13},{6,14},{7,15},{8,0},{9,1},... | collective-permute-start | bytes 49160 | tf_op jit(solution)/shard_map/ppermute | solution.py:30
  64.8 22.6 %collective-permute-start.16 = (f32[2,8,64,128]{3,2,1,0:T(8,128)S(1)}, f32[2,8,64,128]{3,2,1,0:T(8,128)S(1)}, u32[]{:S(2)}, u32[]{:S(2)}) collective-permute-start(f32[2,8,64,128]{3,2,1,0:T(8,128)S(1)} %turn.19.refs_2_.refs_5_), channel_id=1, source_target_pairs={{0,1},{1,2},{2,3},{3,4},{4,5},{5,6},{6,7},{7,8},{8,9},{9,10},{10,1... | collective-permute-start | bytes 1572872 | tf_op jit(solution)/shard_map/ppermute | solution.py:26
  64.8 22.6 %collective-permute-start.17 = (f32[2,8,64,128]{3,2,1,0:T(8,128)S(1)}, f32[2,8,64,128]{3,2,1,0:T(8,128)S(1)}, u32[]{:S(2)}, u32[]{:S(2)}) collective-permute-start(f32[2,8,64,128]{3,2,1,0:T(8,128)S(1)} %turn.19.refs_2_.refs_5_), channel_id=1, source_target_pairs={{0,15},{1,0},{2,1},{3,2},{4,3},{5,4},{6,5},{7,6},{8,7},{9,8},{10,9... | collective-permute-start | bytes 1572872 | tf_op jit(solution)/shard_map/ppermute | solution.py:26
  71.1 29.4 %collective-permute-start.22 = (f32[2,8,64,128]{3,2,1,0:T(8,128)S(1)}, f32[2,8,64,128]{3,2,1,0:T(8,128)S(1)}, u32[]{:S(2)}, u32[]{:S(2)}) collective-permute-start(f32[2,8,64,128]{3,2,1,0:T(8,128)S(1)} %turn.21.refs_2_.refs_5_), channel_id=1, source_target_pairs={{0,1},{1,2},{2,3},{3,4},{4,5},{5,6},{6,7},{7,8},{8,9},{9,10},{10,1... | collective-permute-start | bytes 1572872 | tf_op jit(solution)/shard_map/ppermute | solution.py:26
  71.2 29.4 %collective-permute-start.23 = (f32[2,8,64,128]{3,2,1,0:T(8,128)S(1)}, f32[2,8,64,128]{3,2,1,0:T(8,128)S(1)}, u32[]{:S(2)}, u32[]{:S(2)}) collective-permute-start(f32[2,8,64,128]{3,2,1,0:T(8,128)S(1)} %turn.21.refs_2_.refs_5_), channel_id=1, source_target_pairs={{0,15},{1,0},{2,1},{3,2},{4,3},{5,4},{6,5},{7,6},{8,7},{9,8},{10,9... | collective-permute-start | bytes 1572872 | tf_op jit(solution)/shard_map/ppermute | solution.py:26
  79.6 29.1 %collective-permute-start.20 = (f32[2,8,64,128]{3,2,1,0:T(8,128)S(1)}, f32[2,8,64,128]{3,2,1,0:T(8,128)S(1)}, u32[]{:S(2)}, u32[]{:S(2)}) collective-permute-start(f32[2,8,64,128]{3,2,1,0:T(8,128)S(1)} %turn.20.refs_2_.refs_5_), channel_id=1, source_target_pairs={{0,1},{1,2},{2,3},{3,4},{4,5},{5,6},{6,7},{7,8},{8,9},{9,10},{10,1... | collective-permute-start | bytes 1572872 | tf_op jit(solution)/shard_map/ppermute | solution.py:26
  87.4 22.0 %collective-permute-start.21 = (f32[2,8,64,128]{3,2,1,0:T(8,128)S(1)}, f32[2,8,64,128]{3,2,1,0:T(8,128)S(1)}, u32[]{:S(2)}, u32[]{:S(2)}) collective-permute-start(f32[2,8,64,128]{3,2,1,0:T(8,128)S(1)} %turn.20.refs_2_.refs_5_), channel_id=1, source_target_pairs={{0,15},{1,0},{2,1},{3,2},{4,3},{5,4},{6,5},{7,6},{8,7},{9,8},{10,9... | collective-permute-start | bytes 1572872 | tf_op jit(solution)/shard_map/ppermute | solution.py:26
  89.0 36.1 %collective-permute-start.18 = (f32[2,8,64,128]{3,2,1,0:T(8,128)S(1)}, f32[2,8,64,128]{3,2,1,0:T(8,128)S(1)}, u32[]{:S(2)}, u32[]{:S(2)}) collective-permute-start(f32[2,8,64,128]{3,2,1,0:T(8,128)S(1)} %turn.18.refs_2_.refs_5_), channel_id=1, source_target_pairs={{0,1},{1,2},{2,3},{3,4},{4,5},{5,6},{6,7},{7,8},{8,9},{9,10},{10,1... | collective-permute-start | bytes 1572872 | tf_op jit(solution)/shard_map/ppermute | solution.py:26
  100.6 25.1 %collective-permute-start.19 = (f32[2,8,64,128]{3,2,1,0:T(8,128)S(1)}, f32[2,8,64,128]{3,2,1,0:T(8,128)S(1)}, u32[]{:S(2)}, u32[]{:S(2)}) collective-permute-start(f32[2,8,64,128]{3,2,1,0:T(8,128)S(1)} %turn.18.refs_2_.refs_5_), channel_id=1, source_target_pairs={{0,15},{1,0},{2,1},{3,2},{4,3},{5,4},{6,5},{7,6},{8,7},{9,8},{10,9... | collective-permute-start | bytes 1572872 | tf_op jit(solution)/shard_map/ppermute | solution.py:26
  102.2 28.5 %collective-permute-start.28 = (f32[2,8,64,128]{3,2,1,0:T(8,128)S(1)}, f32[2,8,64,128]{3,2,1,0:T(8,128)S(1)}, u32[]{:S(2)}, u32[]{:S(2)}) collective-permute-start(f32[2,8,64,128]{3,2,1,0:T(8,128)S(1)} %turn.23.refs_2_.refs_5_), channel_id=1, source_target_pairs={{0,1},{1,2},{2,3},{3,4},{4,5},{5,6},{6,7},{7,8},{8,9},{9,10},{10,1... | collective-permute-start | bytes 1572872 | tf_op jit(solution)/shard_map/ppermute | solution.py:26
  108.8 23.7 %collective-permute-start.29 = (f32[2,8,64,128]{3,2,1,0:T(8,128)S(1)}, f32[2,8,64,128]{3,2,1,0:T(8,128)S(1)}, u32[]{:S(2)}, u32[]{:S(2)}) collective-permute-start(f32[2,8,64,128]{3,2,1,0:T(8,128)S(1)} %turn.23.refs_2_.refs_5_), channel_id=1, source_target_pairs={{0,15},{1,0},{2,1},{3,2},{4,3},{5,4},{6,5},{7,6},{8,7},{9,8},{10,9... | collective-permute-start | bytes 1572872 | tf_op jit(solution)/shard_map/ppermute | solution.py:26
  111.0 23.6 %collective-permute-start.26 = (f32[2,8,64,128]{3,2,1,0:T(8,128)S(1)}, f32[2,8,64,128]{3,2,1,0:T(8,128)S(1)}, u32[]{:S(2)}, u32[]{:S(2)}) collective-permute-start(f32[2,8,64,128]{3,2,1,0:T(8,128)S(1)} %turn.22.refs_2_.refs_5_), channel_id=1, source_target_pairs={{0,1},{1,2},{2,3},{3,4},{4,5},{5,6},{6,7},{7,8},{8,9},{9,10},{10,1... | collective-permute-start | bytes 1572872 | tf_op jit(solution)/shard_map/ppermute | solution.py:26
  125.1 9.5 %collective-permute-start.27 = (f32[2,8,64,128]{3,2,1,0:T(8,128)S(1)}, f32[2,8,64,128]{3,2,1,0:T(8,128)S(1)}, u32[]{:S(2)}, u32[]{:S(2)}) collective-permute-start(f32[2,8,64,128]{3,2,1,0:T(8,128)S(1)} %turn.22.refs_2_.refs_5_), channel_id=1, source_target_pairs={{0,15},{1,0},{2,1},{3,2},{4,3},{5,4},{6,5},{7,6},{8,7},{9,8},{10,9... | collective-permute-start | bytes 1572872 | tf_op jit(solution)/shard_map/ppermute | solution.py:26
  127.3 11.5 %collective-permute-start.24 = (f32[2,8,64,128]{3,2,1,0:T(8,128)S(1)}, f32[2,8,64,128]{3,2,1,0:T(8,128)S(1)}, u32[]{:S(2)}, u32[]{:S(2)}) collective-permute-start(f32[2,8,64,128]{3,2,1,0:T(8,128)S(1)} %turn.17.refs_2_), channel_id=1, source_target_pairs={{0,1},{1,2},{2,3},{3,4},{4,5},{5,6},{6,7},{7,8},{8,9},{9,10},{10,1... | collective-permute-start | bytes 1572872 | tf_op jit(solution)/shard_map/ppermute | solution.py:26
  130.7 8.1 %collective-permute-start.25 = (f32[2,8,64,128]{3,2,1,0:T(8,128)S(1)}, f32[2,8,64,128]{3,2,1,0:T(8,128)S(1)}, u32[]{:S(2)}, u32[]{:S(2)}) collective-permute-start(f32[2,8,64,128]{3,2,1,0:T(8,128)S(1)} %turn.17.refs_2_), channel_id=1, source_target_pairs={{0,15},{1,0},{2,1},{3,2},{4,3},{5,4},{6,5},{7,6},{8,7},{9,8},{10,9... | collective-permute-start | bytes 1572872 | tf_op jit(solution)/shard_map/ppermute | solution.py:26
  141.4 13.7 %collective-permute-start.30 = (f32[64,64]{1,0:T(8,128)S(1)}, f32[64,64]{1,0:T(8,128)S(1)}, u32[]{:S(2)}, u32[]{:S(2)}) collective-permute-start(f32[64,64]{1,0:T(8,128)S(1)} %slice_add_fusion.1), channel_id=1, source_target_pairs={{0,1},{1,0},{2,3},{3,2},{4,5},{5,4},{6,7},{7,6},{8,9},{9,8},{10,11... | collective-permute-start | bytes 49160 | tf_op jit(solution)/shard_map/ppermute | solution.py:30
  155.2 4.0 %collective-permute-start.31 = (f32[64,64]{1,0:T(8,128)S(1)}, f32[64,64]{1,0:T(8,128)S(1)}, u32[]{:S(2)}, u32[]{:S(2)}) collective-permute-start(f32[64,64]{1,0:T(8,128)S(1)} %fusion.12), channel_id=1, source_target_pairs={{0,2},{1,3},{2,0},{3,1},{4,6},{5,7},{6,4},{7,5},{8,10},{9,11},{10,... | collective-permute-start | bytes 49160 | tf_op jit(solution)/shard_map/ppermute | solution.py:30
  159.1 3.9 %collective-permute-start.32 = (f32[64,64]{1,0:T(8,128)S(1)}, f32[64,64]{1,0:T(8,128)S(1)}, u32[]{:S(2)}, u32[]{:S(2)}) collective-permute-start(f32[64,64]{1,0:T(8,128)S(1)} %add.92), channel_id=1, source_target_pairs={{0,4},{1,5},{2,6},{3,7},{4,0},{5,1},{6,2},{7,3},{8,12},{9,13},{10,... | collective-permute-start | bytes 49160 | tf_op jit(solution)/shard_map/ppermute | solution.py:30
  163.1 5.1 %collective-permute-start.33 = (f32[64,64]{1,0:T(8,128)S(1)}, f32[64,64]{1,0:T(8,128)S(1)}, u32[]{:S(2)}, u32[]{:S(2)}) collective-permute-start(f32[64,64]{1,0:T(8,128)S(1)} %add.93), channel_id=1, source_target_pairs={{0,8},{1,9},{2,10},{3,11},{4,12},{5,13},{6,14},{7,15},{8,0},{9,1},... | collective-permute-start | bytes 49160 | tf_op jit(solution)/shard_map/ppermute | solution.py:30
